TPU v7x, 256 devices: a whole 4x4x8 slice. The times are simulated.
256 devices in a mesh: row: 16 (over z, core), col: 16 (over y, x).
Axes of the slice: x: 4, y: 4, z: 8, core: 2. Of those that a mesh axis runs over, the one named last changes fastest.
Arguments:
- start_block: float32 [4096, 64, 128], P(('row', 'col')), may hold values from -2700 to 2700
- tile_values: bfloat16 [65536, 128, 128], P(('row', 'col')), may hold values from -3.535534 to 3.535534
- tile_rows: int32 [65536], P(('row', 'col')), may hold values from 0 to 15
- tile_cols: int32 [65536], P(('row', 'col')), may hold values from 0 to 79
- tile_count: int32 [256], P(('row', 'col')), may hold values from 32 to 256, as said below
- send_rows: int32 [256, 256, 32], P(('row', 'col')), may hold values from 0 to 2047
- send_count: int32 [256, 256], P(('row', 'col')), may hold values from 16 to 32, as said below
- rotation: float32 [192, 64], replicated, may hold values from -0.4375 to 0.4375
Outputs:
- embedding: float32 [4096, 64, 128], P(('row', 'col'))
Inputs may be any that keep to these rules, and one draw needn't show every extreme that they name: `tile_cols`: source tiles below 16 are the partition's own row tiles, the others its halo tiles. `tile_count`: slots at or past the count are ignored; some partition fills all 256 slots. `send_count`: slots at or past the count carry zeros; every partition fills all 32 slots for some peer, and some partition receives 32 rows from every partition.
All inputs are finite; a program needn't handle non-finite values.
Results may differ from a plain program's by a relative error of at most 0.0029.
Values may be sent and summed in bfloat16 or wider, within the bound.
A program may use at most 64 MiB of HBM per device.

v0:
```python
import jax
import jax.numpy as jnp
from jax import lax
from jax.sharding import PartitionSpec as P

HIGHEST_PRECISION = lax.Precision.HIGHEST


def local_inner(left_block, right_block):
    return jnp.einsum("tai,tbi->ab", left_block, right_block, precision=HIGHEST_PRECISION)


def unit_columns(product_block, gram_matrix):
    factor = jnp.linalg.cholesky(gram_matrix)
    inverse = lax.linalg.triangular_solve(
        factor, jnp.eye(factor.shape[0], dtype=jnp.float32), left_side=True, lower=True
    )
    return jnp.einsum("ab,tbi->tai", inverse, product_block, precision=HIGHEST_PRECISION)


def apply_graph(current, tile_values, tile_rows, tile_cols, tile_count, send_rows, send_count):
    row_tiles, block_width, tile_size = current.shape
    rounded = current.astype(jnp.bfloat16)
    node_rows = rounded.transpose(0, 2, 1).reshape(row_tiles * tile_size, block_width)
    targets = send_rows[0]
    partitions, capacity = targets.shape
    chosen = node_rows[targets.reshape(-1)].reshape(partitions, capacity, block_width)
    kept_slots = jnp.arange(capacity, dtype=jnp.int32)[None, :] < send_count[0][:, None]
    chosen = jnp.where(kept_slots[:, :, None], chosen, jnp.zeros_like(chosen))
    outgoing = chosen.reshape(lax.axis_size("row"), lax.axis_size("col"), capacity * block_width)
    incoming = lax.all_to_all(
        lax.all_to_all(outgoing, "row", split_axis=0, concat_axis=0, tiled=True),
        "col",
        split_axis=1,
        concat_axis=1,
        tiled=True,
    )
    halo_count = partitions * capacity // tile_size
    halo_block = incoming.reshape(halo_count, tile_size, block_width).transpose(0, 2, 1)
    source = jnp.concatenate([rounded, halo_block], 0)
    picked = source[tile_cols]
    products = jnp.einsum("kbj,kij->kbi", picked, tile_values, preferred_element_type=jnp.float32)
    slot_total = tile_cols.shape[0]
    live_slots = jnp.arange(slot_total, dtype=jnp.int32) < tile_count[0]
    owner_table = (
        tile_rows[None, :] == jnp.arange(row_tiles, dtype=jnp.int32)[:, None]
    ) & live_slots[None, :]
    return jnp.einsum(
        "rk,kbi->rbi", owner_table.astype(jnp.float32), products, precision=HIGHEST_PRECISION
    )


def body(
    start_block, tile_values, tile_rows, tile_cols, tile_count, send_rows, send_count, rotation
):
    node_total = (
        start_block.shape[0] * start_block.shape[2] * lax.axis_size("row") * lax.axis_size("col")
    )
    start_sum = lax.psum(local_inner(start_block, start_block), ("row", "col"))
    vectors = [unit_columns(start_block, start_sum / node_total)]
    for krylov_step in range(2):
        product_block = apply_graph(
            vectors[-1], tile_values, tile_rows, tile_cols, tile_count, send_rows, send_count
        )
        stacked = jnp.concatenate(vectors, 1)
        coefficients = lax.psum(local_inner(stacked, product_block), ("row", "col")) / node_total
        residual_block = product_block - jnp.einsum(
            "ab,tai->tbi", coefficients, stacked, precision=HIGHEST_PRECISION
        )
        gram_matrix = (
            lax.psum(local_inner(residual_block, residual_block), ("row", "col")) / node_total
        )
        vectors.append(unit_columns(residual_block, gram_matrix))
    all_vectors = jnp.concatenate(vectors, 1)
    return jnp.einsum("jb,tji->tbi", rotation, all_vectors, precision=HIGHEST_PRECISION)


def solution(mesh):
    return jax.shard_map(
        body,
        mesh=mesh,
        in_specs=(
            P(("row", "col"), None, None),
            P(("row", "col"), None, None),
            P(("row", "col")),
            P(("row", "col")),
            P(("row", "col")),
            P(("row", "col"), None, None),
            P(("row", "col"), None),
            P(),
        ),
        out_specs=P(("row", "col"), None, None),
        check_vma=False,
    )
```

profile of v0, /device:TPU:1, one launch (start us, length us, event | category | flops | bytes accessed | tf_op | source)
XLA Modules:
  0.0 668.4 jit_solution(7324829424072807957)
XLA Ops:
  1.6 81.5 %psum.35 = f32[64,64]{0,1:T(8,128)S(1)} all-reduce(f32[64,64]{0,1:T(8,128)S(1)} %convolution_bitcast_fusion.8), channel_id=1, replica_groups=mesh['row'=16,'col'=16] {'row','col'}, use_global_device_ids=true, to_apply=%region_0.0 | all-reduce | flops 4096 | bytes 32768 | tf_op jit(solution)/shard_map/psum | solution.py:59
  83.2 5.8 cholesky.59
  90.4 4.9 custom-call.7
  96.8 24.0 %gather_fusion = bf16[8192,64]{1,0:T(8,128)(2,1)S(1)} fusion(bf16[2048,64]{1,0:T(8,128)(2,1)S(1)} %bitcast.92, s32[8192]{0:T(1024)S(1)} %broadcast_clamp_fusion), kind=kCustom, calls=%fused_computation | custom fusion | bytes 2129920 | tf_op jit(solution)/shard_map/gather | solution.py:27
  120.9 2.4 reshape.93
  123.4 2.1 broadcast_in_dim.16
  128.8 33.5 %all_to_all.20 = bf16[16,16,2048]{2,1,0:T(8,128)(2,1)S(1)} all-to-all(bf16[16,16,2048]{2,1,0:T(8,128)(2,1)S(1)} %broadcast_select_fusion.1), channel_id=1, replica_groups=mesh['row'=16,'col'=16] {'row'}, dimensions={0} | all-to-all | bytes 2097152 | tf_op jit(solution)/shard_map/all_to_all | solution.py:32
  163.9 3.9 all-to-all-start.1
  168.7 16.5 %all-to-all-done.1 = bf16[16,16,2048]{2,0,1:T(8,128)(2,1)S(1)} async-done(((bf16[16,16,2048]{2,0,1:T(8,128)(2,1)}), bf16[16,16,2048]{2,0,1:T(8,128)(2,1)S(1)}, u32[]{:S(2)}, u32[]{:S(2)}) %all-to-all-start.1) | async-done | bytes 1048608 | tf_op jit(solution)/shard_map/all_to_all | solution.py:31
  186.8 3.3 reshape.94
  190.2 2.1 pad_maximum_fusion
  192.2 10.4 %gather_fusion.1 = bf16[256,64,128]{1,2,0:T(8,128)(2,1)} fusion(bf16[80,64,128]{1,2,0:T(8,128)(2,1)} %pad_maximum_fusion, s32[1024]{0:T(1024)S(1)} %pad_clamp_fusion), kind=kCustom, calls=%fused_computation.1 | custom fusion | bytes 8389632 | tf_op jit(solution)/shard_map/gather | solution.py:41
  202.6 9.7 %fusion.57 = f32[256,64,128]{2,1,0:T(8,128)S(1)} fusion(bf16[256,64,128]{1,2,0:T(8,128)(2,1)} %gather_fusion.1, bf16[256,128,128]{2,1,0:T(8,128)(2,1)} %param.12), kind=kOutput, calls=%fused_computation.100 | convolution fusion | flops 536870912 | bytes 20971520 | tf_op jit(solution)/shard_map/kbj,kij->kbi/dot_general | solution.py:42
  212.3 7.5 %fusion.2 = f32[16,64,128]{2,0,1:T(8,128)S(1)} fusion(f32[256,64,128]{2,1,0:T(8,128)S(1)} %fusion.57, s32[256]{0:T(256)S(1)} %copy-done.6, pred[256]{0:T(512)(128)(4,1)S(1)} %iota_compare_fusion.7), kind=kOutput, calls=%fused_computation.6 | convolution fusion | flops 402661376 | bytes 8914176 | tf_op jit(solution)/shard_map/rk,kbi->rbi/dot_general | solution.py:48
  220.5 72.7 %psum.36 = f32[64,64]{0,1:T(8,128)S(1)} all-reduce(f32[64,64]{0,1:T(8,128)S(1)} %convolution_bitcast_fusion.6), channel_id=1, replica_groups=mesh['row'=16,'col'=16] {'row','col'}, use_global_device_ids=true, to_apply=%region_3.0 | all-reduce | flops 4096 | bytes 32768 | tf_op jit(solution)/shard_map/psum | solution.py:66
  295.0 73.9 %psum.37 = f32[64,64]{0,1:T(8,128)S(1)} all-reduce(f32[64,64]{0,1:T(8,128)S(1)} %convolution_bitcast_fusion.5), channel_id=1, replica_groups=mesh['row'=16,'col'=16] {'row','col'}, use_global_device_ids=true, to_apply=%region_4.0 | all-reduce | flops 4096 | bytes 32768 | tf_op jit(solution)/shard_map/psum | solution.py:71
  369.0 5.8 cholesky.70
  376.3 4.9 custom-call.8
  383.4 24.0 %gather_fusion.2 = bf16[8192,64]{1,0:T(8,128)(2,1)S(1)} fusion(bf16[2048,64]{1,0:T(8,128)(2,1)S(1)} %bitcast.93, s32[8192]{0:T(1024)S(1)} %broadcast_clamp_fusion), kind=kCustom, calls=%fused_computation.2 | custom fusion | bytes 2129920 | tf_op jit(solution)/shard_map/gather | solution.py:27
  407.4 2.4 reshape.96
  411.3 32.6 %all_to_all.21 = bf16[16,16,2048]{2,1,0:T(8,128)(2,1)S(1)} all-to-all(bf16[16,16,2048]{2,1,0:T(8,128)(2,1)S(1)} %broadcast_select_fusion), channel_id=1, replica_groups=mesh['row'=16,'col'=16] {'row'}, dimensions={0} | all-to-all | bytes 2097152 | tf_op jit(solution)/shard_map/all_to_all | solution.py:32
  445.5 3.9 all-to-all-start.3
  449.7 18.4 %all-to-all-done.3 = bf16[16,16,2048]{2,0,1:T(8,128)(2,1)S(1)} async-done(((bf16[16,16,2048]{2,0,1:T(8,128)(2,1)}), bf16[16,16,2048]{2,0,1:T(8,128)(2,1)S(1)}, u32[]{:S(2)}, u32[]{:S(2)}) %all-to-all-start.3) | async-done | bytes 1048608 | tf_op jit(solution)/shard_map/all_to_all | solution.py:31
  469.7 3.3 reshape.97
  473.0 2.1 pad_maximum_fusion.1
  475.1 10.4 %gather_fusion.3 = bf16[256,64,128]{1,2,0:T(8,128)(2,1)} fusion(bf16[80,64,128]{1,2,0:T(8,128)(2,1)} %pad_maximum_fusion.1, s32[1024]{0:T(1024)S(1)} %pad_clamp_fusion), kind=kCustom, calls=%fused_computation.3 | custom fusion | bytes 8389632 | tf_op jit(solution)/shard_map/gather | solution.py:41
  485.4 9.5 %fusion.58 = f32[256,64,128]{2,1,0:T(8,128)S(1)} fusion(bf16[256,64,128]{1,2,0:T(8,128)(2,1)} %gather_fusion.3, bf16[256,128,128]{2,1,0:T(8,128)(2,1)} %param.12), kind=kOutput, calls=%fused_computation.101 | convolution fusion | flops 536870912 | bytes 20971520 | tf_op jit(solution)/shard_map/kbj,kij->kbi/dot_general | solution.py:42
  495.0 7.5 %fusion = f32[16,64,128]{2,0,1:T(8,128)S(1)} fusion(f32[256,64,128]{2,1,0:T(8,128)S(1)} %fusion.58, s32[256]{0:T(256)S(1)} %copy-done.6, pred[256]{0:T(512)(128)(4,1)S(1)} %iota_compare_fusion.7), kind=kOutput, calls=%fused_computation.4 | convolution fusion | flops 402661376 | bytes 8914176 | tf_op jit(solution)/shard_map/rk,kbi->rbi/dot_general | solution.py:48
  503.7 72.8 %psum.38 = f32[128,64]{0,1:T(8,128)S(1)} all-reduce(f32[128,64]{0,1:T(8,128)S(1)} %convolution_bitcast_fusion.1), channel_id=1, replica_groups=mesh['row'=16,'col'=16] {'row','col'}, use_global_device_ids=true, to_apply=%region_5.8 | all-reduce | flops 8192 | bytes 65536 | tf_op jit(solution)/shard_map/psum | solution.py:66
  578.3 74.5 %psum.39 = f32[64,64]{0,1:T(8,128)S(1)} all-reduce(f32[64,64]{0,1:T(8,128)S(1)} %convolution_bitcast_fusion.3), channel_id=1, replica_groups=mesh['row'=16,'col'=16] {'row','col'}, use_global_device_ids=true, to_apply=%region_6.9 | all-reduce | flops 4096 | bytes 32768 | tf_op jit(solution)/shard_map/psum | solution.py:71
  652.9 5.8 cholesky.81
  660.1 4.9 custom-call.9
  (72 shorter events, 29.6 us)
Async XLA Ops:
  0.0 1.0 copy-start
  0.0 96.5 %copy-start.5 = (s32[1,256,32]{1,2,0:T(8,128)S(1)}, s32[1,256,32]{1,2,0:T(8,128)}, u32[]{:S(2)}) copy-start(s32[1,256,32]{1,2,0:T(8,128)} %param.16) | copy-start | bytes 98308
  96.8 26.5 %copy-start.7 = (s32[1,256]{1,0:T(1,128)S(1)}, s32[1,256]{1,0:T(1,128)}, u32[]{:S(2)}) copy-start(s32[1,256]{1,0:T(1,128)} %param.17) | copy-start | bytes 3076
  127.3 36.6 %copy-start.3 = (pred[16,16,2048]{2,1,0:T(8,128)(4,1)}, pred[16,16,2048]{2,1,0:T(8,128)(4,1)S(1)}, u32[]{:S(2)}) copy-start(pred[16,16,2048]{2,1,0:T(8,128)(4,1)S(1)} %broadcast_in_dim.17) | copy-start | bytes 1572868
  128.8 39.9 %copy-start.8 = (s32[256]{0:T(256)S(1)}, s32[256]{0:T(256)}, u32[]{:S(2)}) copy-start(s32[256]{0:T(256)} %param.14) | copy-start | bytes 3076
  163.9 21.4 %all-to-all-start.1 = ((bf16[16,16,2048]{2,0,1:T(8,128)(2,1)}), bf16[16,16,2048]{2,0,1:T(8,128)(2,1)S(1)}, u32[]{:S(2)}, u32[]{:S(2)}) async-start(bf16[16,16,2048]{2,0,1:T(8,128)(2,1)} %copy.49), calls=%async_computation.1 | async-start | bytes 2097152 | tf_op jit(solution)/shard_map/all_to_all | solution.py:31
  202.6 9.7 %copy-start.6 = (s32[256]{0:T(256)S(1)}, s32[256]{0:T(256)}, u32[]{:S(2)}) copy-start(s32[256]{0:T(256)} %param.13) | copy-start | bytes 3076
  445.5 22.6 %all-to-all-start.3 = ((bf16[16,16,2048]{2,0,1:T(8,128)(2,1)}), bf16[16,16,2048]{2,0,1:T(8,128)(2,1)S(1)}, u32[]{:S(2)}, u32[]{:S(2)}) async-start(bf16[16,16,2048]{2,0,1:T(8,128)(2,1)} %copy.64), calls=%async_computation.3 | async-start | bytes 2097152 | tf_op jit(solution)/shard_map/all_to_all | solution.py:31
  495.0 7.5 %copy-start.2 = (f32[16,128,64]{1,2,0:T(8,128)S(1)}, f32[16,128,64]{1,2,0:T(8,128)}, u32[]{:S(2)}) copy-start(f32[16,128,64]{1,2,0:T(8,128)} %get-tuple-element.11) | copy-start | bytes 1572868
  502.5 163.6 %copy-start.4 = (f32[192,64]{0,1:T(8,128)S(1)}, f32[192,64]{0,1:T(8,128)}, u32[]{:S(2)}) copy-start(f32[192,64]{0,1:T(8,128)} %param.18) | copy-start | bytes 147460
  502.5 165.5 %copy-start.1 = (f32[16,64,128]{2,1,0:T(8,128)S(1)}, f32[16,64,128]{2,1,0:T(8,128)}, u32[]{:S(2)}) copy-start(f32[16,64,128]{2,1,0:T(8,128)} %param.11) | copy-start | bytes 1572868
where the time goes:
time: 675 us; the launch traced here: 668 us
  blocking collectives  442 us (65%)
  local copies, waits for them, and re-layouts  93.1 us (14%)
  matrix products  45.1 us (7%)
  other arithmetic  44.5 us (7%)
  waiting for transfers between devices  35 us (5%)
  starting transfers between devices  7.72 us (1%)
    psum x2, blocking collectives, body(): lax.psum(local_inner(residual_block, residual_block), ('row', 'col'))  148 us
    psum x2, blocking collectives, body(): lax.psum(local_inner(stacked, product_block), ('row', 'col')) / node_total  146 us
    psum x1, blocking collectives, body(): start_sum = lax.psum(local_inner(start_block, start_block), ('row', 'col'))  81.5 us
    all_to_all x2, blocking collectives, apply_graph(): lax.all_to_all(outgoing, 'row', split_axis=0, concat_axis=0, tiled=True)  66.1 us
    gather x2, local copies, waits for them, and re-layouts, apply_graph(): node_rows[targets.reshape(-1)].reshape(partitions, capacity, block_width)  48.1 us
    all_to_all x2, waiting for transfers between devices, apply_graph(): lax.all_to_all(lax.all_to_all(outgoing, 'row', split_axis=0, concat_axis=...  35 us
    gather x2, local copies, waits for them, and re-layouts, apply_graph(): picked = source[tile_cols]  20.7 us
    another operation x9, other arithmetic, unit_columns(): factor = jnp.linalg.cholesky(gram_matrix)  19.6 us
  transfers between devices with their start and end apart: 2, of which 2 were waited for; matrix products, arithmetic and copies ran while one was open for 0% of the time, Pallas kernels for 0%

commit v1 on v0

v1 whole, which is shorter than its diff:
```python
import functools

import jax
import jax.numpy as jnp
from jax import lax
from jax.experimental import pallas as pl
from jax.experimental.pallas import tpu as pltpu
from jax.sharding import PartitionSpec as P

MESH = pl.DeviceIdType.MESH
HIGHEST = lax.Precision.HIGHEST
F32 = jnp.float32
BF16 = jnp.bfloat16
RT = 16
BLK = 64
TILE = 128
DEVS = 256
NODES = 524288
CHUNK = 16
VMEM = pl.BlockSpec(memory_space=pltpu.VMEM)
SMEM = pl.BlockSpec(memory_space=pltpu.SMEM)


def ar_kernel(x_ref, o_ref, pbuf, xybuf, zbuf, fin, ss, rs):
    row = lax.axis_index("row")
    col = lax.axis_index("col")
    core = lax.rem(row, 2)
    z = row // 2
    prow = row + 1 - 2 * core
    half = x_ref.shape[0] // 2
    bar = pltpu.get_barrier_semaphore()
    pl.semaphore_signal(bar, inc=1, device_id=(prow, col), device_id_type=MESH)

    def greet_xy(i, c):
        pl.semaphore_signal(bar, inc=1, device_id=(row, lax.rem(col + i, 16)), device_id_type=MESH)
        return c

    lax.fori_loop(1, 16, greet_xy, 0)

    def greet_z(i, c):
        pl.semaphore_signal(bar, inc=1, device_id=(lax.rem(row + 2 * i, 16), col), device_id_type=MESH)
        return c

    lax.fori_loop(1, 8, greet_z, 0)
    pl.semaphore_wait(bar, 23)
    mine = pl.ds(pl.multiple_of(core * half, half), half)
    other = pl.ds(pl.multiple_of((1 - core) * half, half), half)
    cp = pltpu.make_async_remote_copy(
        x_ref.at[other], pbuf, ss.at[0], rs.at[0], device_id=(prow, col), device_id_type=MESH
    )
    cp.start()
    cp.wait()
    xybuf[col] = x_ref[mine, :] + pbuf[...]

    def send_xy(i, c):
        pltpu.make_async_remote_copy(
            xybuf.at[col], xybuf.at[col], ss.at[1], rs.at[1],
            device_id=(row, lax.rem(col + i, 16)), device_id_type=MESH,
        ).start()
        return c

    lax.fori_loop(1, 16, send_xy, 0)
    w = pltpu.make_async_remote_copy(
        xybuf.at[pl.ds(0, 15)], xybuf.at[pl.ds(0, 15)], ss.at[1], rs.at[1],
        device_id=(prow, col), device_id_type=MESH,
    )
    w.wait_recv()
    w.wait_send()
    zbuf[z] = jnp.sum(xybuf[...], axis=0)

    def send_z(i, c):
        pltpu.make_async_remote_copy(
            zbuf.at[z], zbuf.at[z], ss.at[2], rs.at[2],
            device_id=(lax.rem(row + 2 * i, 16), col), device_id_type=MESH,
        ).start()
        return c

    lax.fori_loop(1, 8, send_z, 0)
    w = pltpu.make_async_remote_copy(
        zbuf.at[pl.ds(0, 7)], zbuf.at[pl.ds(0, 7)], ss.at[2], rs.at[2],
        device_id=(prow, col), device_id_type=MESH,
    )
    w.wait_recv()
    w.wait_send()
    fin[mine, :] = jnp.sum(zbuf[...], axis=0)
    cp = pltpu.make_async_remote_copy(
        fin.at[mine], fin.at[mine], ss.at[3], rs.at[3], device_id=(prow, col), device_id_type=MESH
    )
    cp.start()
    cp.wait()
    o_ref[...] = fin[...]


def allreduce(x):
    rows = x.shape[0]
    half = rows // 2
    return pl.pallas_call(
        ar_kernel,
        out_shape=jax.ShapeDtypeStruct(x.shape, F32),
        in_specs=[VMEM],
        out_specs=VMEM,
        scratch_shapes=[
            pltpu.VMEM((half, 128), F32),
            pltpu.VMEM((16, half, 128), F32),
            pltpu.VMEM((8, half, 128), F32),
            pltpu.VMEM((rows, 128), F32),
            pltpu.SemaphoreType.DMA((4,)),
            pltpu.SemaphoreType.DMA((4,)),
        ],
        compiler_params=pltpu.CompilerParams(collective_id=rows // 32, has_side_effects=True),
    )(x)


def ex_kernel(s_ref, o_ref, ss, rs, ls):
    row = lax.axis_index("row")
    col = lax.axis_index("col")
    me = row * 16 + col
    lc = pltpu.make_async_copy(s_ref.at[me], o_ref.at[me], ls)
    lc.start()

    def go(i, c):
        r2 = lax.rem(row + lax.rem(i, 16), 16)
        c2 = lax.rem(col + i // 16, 16)
        pltpu.make_async_remote_copy(
            s_ref.at[r2 * 16 + c2], o_ref.at[me], ss, rs, device_id=(r2, c2), device_id_type=MESH
        ).start()
        return c

    lax.fori_loop(1, 256, go, 0)
    w = pltpu.make_async_remote_copy(
        s_ref.at[pl.ds(0, 255)], o_ref.at[pl.ds(0, 255)], ss, rs,
        device_id=(row, lax.rem(col + 1, 16)), device_id_type=MESH,
    )
    w.wait_recv()
    w.wait_send()
    lc.wait()


def exchange(x):
    return pl.pallas_call(
        ex_kernel,
        out_shape=jax.ShapeDtypeStruct(x.shape, x.dtype),
        in_specs=[VMEM],
        out_specs=VMEM,
        scratch_shapes=[pltpu.SemaphoreType.DMA] * 3,
        compiler_params=pltpu.CompilerParams(has_side_effects=True),
    )(x)


def nt(a, b):
    return lax.dot_general(a, b, (((1,), (1,)), ((), ())), precision=HIGHEST, preferred_element_type=F32)


def nn(a, b):
    return lax.dot_general(a, b, (((1,), (0,)), ((), ())), precision=HIGHEST, preferred_element_type=F32)


def wide(ref):
    return jnp.concatenate([ref[t] for t in range(RT)], axis=1)


def put_wide(ref, x):
    for t in range(RT):
        ref[t] = x[:, t * TILE:(t + 1) * TILE].astype(ref.dtype)


def fold(g):
    return jnp.concatenate([g[:32], g[32:]], axis=1)


def unfold(p):
    return jnp.concatenate([p[:, :64], p[:, 64:]], axis=0)


def inverse_factor(g):
    lane = lax.broadcasted_iota(jnp.int32, (8, 128), 1)
    sub = lax.broadcasted_iota(jnp.int32, (8, 128), 0)
    wide_g = jnp.concatenate([g, jnp.zeros((64, 64), F32)], axis=1)
    blocks = [
        jnp.where(lane == sub + (64 + 8 * b), 1.0, wide_g[8 * b:8 * b + 8]) for b in range(8)
    ]
    for j in range(64):
        jb, jr = divmod(j, 8)
        pivot_row = blocks[jb][jr:jr + 1, :]
        scaled = pivot_row / pivot_row[:, j:j + 1]
        for b in range(jb, 8):
            c = blocks[b][:, j:j + 1]
            if b == jb:
                c = jnp.where(sub[:, :1] > jr, c, 0.0)
            blocks[b] = blocks[b] - c * scaled
    out = []
    for b in range(8):
        d = jnp.sum(jnp.where(lane == sub + 8 * b, blocks[b], 0.0), axis=1, keepdims=True)
        out.append(blocks[b][:, 64:] / jnp.sqrt(d))
    return jnp.concatenate(out, axis=0)


def swap_groups(parts):
    lane = lax.broadcasted_iota(jnp.int32, (16, 128), 1)
    low = lane < 64
    even = lax.rem(lane, 64) < 32
    first = {}
    for g in range(2):
        a, b = parts[g], parts[g + 2]
        first[0, g] = jnp.where(low, a, pltpu.roll(b, 64, 1))
        first[1, g] = jnp.where(low, pltpu.roll(a, 64, 1), b)
    out = []
    for h in range(2):
        a, b = first[h, 0], first[h, 1]
        out.append(jnp.where(even, a, pltpu.roll(b, 32, 1)))
        out.append(jnp.where(even, pltpu.roll(a, 96, 1), b))
    return out


def gram_kernel(x_ref, o_ref):
    x = wide(x_ref)
    o_ref[...] = fold(nt(x, x))


def ortho_kernel(z_ref, g_ref, l_ref, t_ref, q_ref, p_ref, s_ref, lhs):
    m = inverse_factor(unfold(g_ref[...]) * (1.0 / NODES))
    put_wide(q_ref, nn(m, wide(z_ref)))
    for t in range(RT):
        p_ref[t] = q_ref[t].astype(BF16)
        lhs[64 * (t // 2):64 * (t // 2) + 64, 128 * (t % 2):128 * (t % 2) + 128] = q_ref[t].astype(BF16)
    node = lax.broadcasted_iota(jnp.int32, (256, 256), 0)

    def chunk(c, carry):
        lsel = jnp.concatenate([l_ref[pl.ds(2 * c, 1), :], l_ref[pl.ds(2 * c + 1, 1), :]], axis=1)
        tsel = jnp.concatenate([t_ref[pl.ds(2 * c, 1), :], t_ref[pl.ds(2 * c + 1, 1), :]], axis=1)
        hot = jnp.where(node == lsel, 1.0, 0.0).astype(BF16)
        r = jnp.dot(lhs[...], hot, preferred_element_type=F32)
        acc = jnp.zeros((64, 256), F32)
        for t in range(8):
            acc = acc + jnp.where(tsel == t, r[64 * t:64 * t + 64], 0.0)
        for h in range(2):
            msgs = swap_groups([acc[16 * g:16 * g + 16, 128 * h:128 * h + 128] for g in range(4)])
            for q in range(4):
                s_ref[8 * c + 4 * h + q] = msgs[q].astype(BF16)
        return carry

    lax.fori_loop(0, 32, chunk, 0)


def apply_kernel(nb, *refs):
    rows, cols, count, values, p_ref, h_ref = refs[:6]
    basis = refs[6:6 + nb]
    y_ref, c_ref, src, acc, buf, sem = refs[6 + nb:]
    n = count[0]
    nchunk = (n + CHUNK - 1) // CHUNK

    def fetch(c):
        slot = lax.rem(c, 3)
        return pltpu.make_async_copy(values.at[pl.ds(c * CHUNK, CHUNK)], buf.at[slot], sem.at[slot])

    fetch(0).start()

    @pl.when(nchunk > 1)
    def _():
        fetch(1).start()

    acc[...] = jnp.zeros_like(acc)
    src[0:RT] = p_ref[...]

    def unpack(h, c):
        parts = swap_groups([h_ref[4 * h + q].astype(F32) for q in range(4)])
        for g in range(4):
            src[RT + h, 16 * g:16 * g + 16, :] = parts[g].astype(BF16)
        return c

    lax.fori_loop(0, 64, unpack, 0)

    def step(c, carry):
        @pl.when(c + 2 < nchunk)
        def _():
            fetch(c + 2).start()

        fetch(c).wait()
        slot = lax.rem(c, 3)
        for u in range(CHUNK):
            k = c * CHUNK + u
            r = jnp.where(k < n, rows[k], RT)
            acc[r] += lax.dot_general(
                src[cols[k]], buf[slot, u], (((1,), (1,)), ((), ())), preferred_element_type=F32
            )
        return carry

    lax.fori_loop(0, nchunk, step, 0)
    y_ref[...] = acc[0:RT]
    y = wide(acc)
    c_ref[...] = jnp.concatenate([fold(nt(y, wide(b))) for b in basis], axis=0)


def project_kernel(nb, *refs):
    y_ref, c_ref = refs[:2]
    basis = refs[2:2 + nb]
    z_ref, g_ref = refs[2 + nb:]
    z = wide(y_ref)
    for i, b in enumerate(basis):
        z = z - nn(unfold(c_ref[32 * i:32 * i + 32]) * (1.0 / NODES), wide(b))
    put_wide(z_ref, z)
    g_ref[...] = fold(nt(z, z))


def final_kernel(z_ref, g_ref, rot_ref, q0_ref, q1_ref, o_ref):
    m = inverse_factor(unfold(g_ref[...]) * (1.0 / NODES))
    rot = rot_ref[...]
    tail = nn(rot[:, 128:192], m)
    o = nn(rot[:, 0:64], wide(q0_ref)) + nn(rot[:, 64:128], wide(q1_ref)) + nn(tail, wide(z_ref))
    put_wide(o_ref, o)


def block(dtype):
    return jax.ShapeDtypeStruct((RT, BLK, TILE), dtype)


def gram(x):
    return pl.pallas_call(
        gram_kernel, out_shape=jax.ShapeDtypeStruct((32, 128), F32), in_specs=[VMEM], out_specs=VMEM
    )(x)


def ortho(z, g, lsel, tsel):
    return pl.pallas_call(
        ortho_kernel,
        out_shape=(block(F32), block(BF16), jax.ShapeDtypeStruct((DEVS, 16, 128), BF16)),
        in_specs=[VMEM] * 4,
        out_specs=(VMEM,) * 3,
        scratch_shapes=[pltpu.VMEM((512, 256), BF16)],
    )(z, g, lsel, tsel)


def apply_graph(rows, cols, count, values, p, halo, basis):
    nb = len(basis)
    return pl.pallas_call(
        functools.partial(apply_kernel, nb),
        out_shape=(block(F32), jax.ShapeDtypeStruct((32 * nb, 128), F32)),
        in_specs=[SMEM] * 3 + [pl.BlockSpec(memory_space=pl.ANY)] + [VMEM] * (2 + nb),
        out_specs=(VMEM,) * 2,
        scratch_shapes=[
            pltpu.VMEM((80, BLK, TILE), BF16),
            pltpu.VMEM((RT + 1, BLK, TILE), F32),
            pltpu.VMEM((3, CHUNK, TILE, TILE), BF16),
            pltpu.SemaphoreType.DMA((3,)),
        ],
    )(rows, cols, count, values, p, halo, *basis)


def project(y, c, basis):
    nb = len(basis)
    return pl.pallas_call(
        functools.partial(project_kernel, nb),
        out_shape=(block(F32), jax.ShapeDtypeStruct((32, 128), F32)),
        in_specs=[VMEM] * (2 + nb),
        out_specs=(VMEM,) * 2,
    )(y, c, *basis)


def body(start, values, rows, cols, count, send_rows, send_count, rotation):
    slot = jnp.arange(32, dtype=jnp.int32)
    wanted = send_rows[0]
    lsel = (wanted % 256).reshape(64, 128)
    tsel = jnp.where(slot[None, :] < send_count[0][:, None], wanted // 256, -1).reshape(64, 128)
    g = allreduce(gram(start))
    q, p, out = ortho(start, g, lsel, tsel)
    basis = [q]
    for k in range(2):
        halo = exchange(out)
        y, c = apply_graph(rows, cols, count, values, p, halo, basis)
        z, g = project(y, allreduce(c), basis)
        g = allreduce(g)
        if k == 0:
            q, p, out = ortho(z, g, lsel, tsel)
            basis.append(q)
    return pl.pallas_call(
        final_kernel, out_shape=block(F32), in_specs=[VMEM] * 5, out_specs=VMEM
    )(z, g, rotation.T, basis[0], basis[1])


def solution(mesh):
    spec = P(("row", "col"))
    return jax.shard_map(
        body,
        mesh=mesh,
        in_specs=(spec,) * 7 + (P(),),
        out_specs=spec,
        check_vma=False,
    )
```

time: 675 us -> 277 us (0.41)
  blocking collectives: 442 us -> 0 us
  Pallas kernels: 0 us -> 270 us
  local copies, waits for them, and re-layouts: 93.1 us -> 1.82 us
  matrix products: 45.1 us -> 0 us
  other arithmetic: 44.5 us -> 2.01 us
  waiting for transfers between devices: 35 us -> 0 us
  starting transfers between devices: 7.72 us -> 0 us
    psum x5 -> x0, blocking collectives: 375 us -> none  [the longest x2 148 us: body(): lax.psum(local_inner(residual_block, residual_block), ('row', 'col'))]
    pallas_call x0 -> x15, Pallas kernels: none -> 270 us  [the longest x5 92.6 us: allreduce(): pl.pallas_call(ar_kernel, out_shape=jax.ShapeDtypeStruct(x.shape, F32), i...]
    gather x4 -> x0, local copies, waits for them, and re-layouts: 68.8 us -> none  [the longest x2 48.1 us: apply_graph(): node_rows[targets.reshape(-1)].reshape(partitions, capacity, block_width)]
    all_to_all x2 -> x0, blocking collectives: 66.1 us -> none  [apply_graph(): lax.all_to_all(outgoing, 'row', split_axis=0, concat_axis=0, tiled=True)]
    dot_general x15 -> x0, matrix products: 44.3 us -> none  [the longest x2 19.2 us: apply_graph(): jnp.einsum('kbj,kij->kbi', picked, tile_values, preferred_element_type=jn...]
    another operation x15 -> x0, other arithmetic: 36.3 us -> none  [the longest x9 19.6 us: unit_columns(): factor = jnp.linalg.cholesky(gram_matrix)]
    all_to_all x2 -> x0, waiting for transfers between devices: 35 us -> none  [apply_graph(): lax.all_to_all(lax.all_to_all(outgoing, 'row', split_axis=0, concat_axis=...]
    reshape x6 -> x0, local copies, waits for them, and re-layouts: 12.1 us -> none  [the longest x2 6.65 us: apply_graph(): incoming.reshape(halo_count, tile_size, block_width).transpose(0, 2, 1)]
  transfers between devices with their start and end apart: 2 -> 0, of which waited for: 2 -> 0; matrix products, arithmetic and copies ran while one was open for 0% -> 0% of each run, Pallas kernels for 0% -> 0%
where the time goes in v1:
time: 277 us; the launch traced here: 275 us
  Pallas kernels  270 us (97%)
    pallas_call x5, Pallas kernels, allreduce(): pl.pallas_call(ar_kernel, out_shape=jax.ShapeDtypeStruct(x.shape, F32), i...  92.6 us
    pallas_call x2, Pallas kernels, exchange(): pl.pallas_call(ex_kernel, out_shape=jax.ShapeDtypeStruct(x.shape, x.dtype...  78.9 us
    pallas_call x2, Pallas kernels, ortho(): pl.pallas_call(ortho_kernel, out_shape=(block(F32), block(BF16), jax.Shap...  40.9 us
    pallas_call x2, Pallas kernels, apply_graph(): pl.pallas_call(functools.partial(apply_kernel, nb), out_shape=(block(F32)...  39.7 us
    pallas_call x1, Pallas kernels, body(): pl.pallas_call(final_kernel, out_shape=block(F32), in_specs=[VMEM] * 5, o...  9.04 us
    pallas_call x2, Pallas kernels, project(): pl.pallas_call(functools.partial(project_kernel, nb), out_shape=(block(F3...  7.11 us

profile of v1, /device:TPU:1, one launch (start us, length us, event | category | flops | bytes accessed | tf_op | source)
XLA Modules:
  0.0 275.0 jit_solution(8723825671765114482)
XLA Ops:
  0.7 0.5 broadcast.32
  1.2 1.3 reduce.3
  2.5 0.1 lt.30
  2.6 2.3 shard_map.82.x_ref
  4.9 23.4 %shard_map.83.g_ref = f32[32,128]{1,0:T(8,128)} custom-call(f32[32,128]{1,0:T(8,128)} %shard_map.82.x_ref), custom_call_target="tpu_custom_call" | custom-call | tf_op jit(solution)/shard_map/pallas_call | solution.py:97
  28.2 0.1 lt.32
  28.3 0.1 copy.11
  28.4 0.1 copy.12
  28.5 0.9 copy.10
  29.4 0.1 squeeze.3
  29.5 0.7 fusion
  30.1 20.4 %shard_map.84 = (f32[16,64,128]{2,1,0:T(8,128)}, bf16[16,64,128]{2,1,0:T(8,128)(2,1)}, bf16[256,16,128]{2,1,0:T(8,128)(2,1)}) custom-call(f32[16,64,128]{2,1,0:T(8,128)} %z_ref.1, f32[32,128]{1,0:T(8,128)} %shard_map.83.g_ref, s32[64,128]{1,0:T(8,128)} %get-tuple-element.34.l_ref, s32[64,128]{1,0:T(8,128)} %get-tuple-element.33.t_ref), custom_call_target="tpu_custom_call" | custom-call | tf_op jit(solution)/shard_map/pallas_call | solution.py:324
  50.6 39.4 %shard_map.85.refs_5_ = bf16[256,16,128]{2,1,0:T(8,128)(2,1)} custom-call(bf16[256,16,128]{2,1,0:T(8,128)(2,1)} %get-tuple-element.20.s_ref), custom_call_target="tpu_custom_call" | custom-call | tf_op jit(solution)/shard_map/pallas_call | solution.py:140
  90.0 19.5 %shard_map.86 = (f32[16,64,128]{2,1,0:T(8,128)}, f32[32,128]{1,0:T(8,128)}) custom-call(s32[256]{0:T(256)} %refs_0_.3, s32[256]{0:T(256)} %refs_1_.3, s32[1]{0:T(128)S(6)} %copy.13.refs_2_, bf16[256,128,128]{2,1,0:T(8,128)(2,1)} %refs_3_.3, bf16[16,64,128]{2,1,0:T(8,128)(2,1)} %get-tuple-element.19.refs_4_, bf16[256,16,128]{2,1,0:T(8,128)(2,1)} %shard_map.85.refs_5_, ...), custom_call_target="tpu_custom_call" | custom-call | tf_op jit(solution)/shard_map/pallas_call | solution.py:335
  109.5 17.7 %shard_map.87.refs_1_ = f32[32,128]{1,0:T(8,128)} custom-call(f32[32,128]{1,0:T(8,128)} %get-tuple-element.23.x_ref), custom_call_target="tpu_custom_call" | custom-call | tf_op jit(solution)/shard_map/pallas_call | solution.py:97
  127.2 3.1 %shard_map.88 = (f32[16,64,128]{2,1,0:T(8,128)}, f32[32,128]{1,0:T(8,128)}) custom-call(f32[16,64,128]{2,1,0:T(8,128)} %get-tuple-element.22.refs_0_, f32[32,128]{1,0:T(8,128)} %shard_map.87.refs_1_, f32[16,64,128]{2,1,0:T(8,128)} %get-tuple-element.21.refs_6_.refs_2_.q0_ref), custom_call_target="tpu_custom_call" | custom-call | tf_op jit(solution)/shard_map/pallas_call | solution.py:351
  130.3 16.1 %shard_map.89.g_ref = f32[32,128]{1,0:T(8,128)} custom-call(f32[32,128]{1,0:T(8,128)} %get-tuple-element.25.x_ref), custom_call_target="tpu_custom_call" | custom-call | tf_op jit(solution)/shard_map/pallas_call | solution.py:97
  146.4 20.4 %shard_map.90 = (f32[16,64,128]{2,1,0:T(8,128)}, bf16[16,64,128]{2,1,0:T(8,128)(2,1)}, bf16[256,16,128]{2,1,0:T(8,128)(2,1)}) custom-call(f32[16,64,128]{2,1,0:T(8,128)} %get-tuple-element.24.z_ref, f32[32,128]{1,0:T(8,128)} %shard_map.89.g_ref, s32[64,128]{1,0:T(8,128)} %get-tuple-element.34.l_ref, s32[64,128]{1,0:T(8,128)} %get-tuple-element.33.t_ref), custom_call_target="tpu_custom_call" | custom-call | tf_op jit(solution)/shard_map/pallas_call | solution.py:324
  166.9 39.4 %shard_map.91.refs_5_ = bf16[256,16,128]{2,1,0:T(8,128)(2,1)} custom-call(bf16[256,16,128]{2,1,0:T(8,128)(2,1)} %get-tuple-element.27.s_ref), custom_call_target="tpu_custom_call" | custom-call | tf_op jit(solution)/shard_map/pallas_call | solution.py:140
  206.3 20.2 %shard_map.92 = (f32[16,64,128]{2,1,0:T(8,128)}, f32[64,128]{1,0:T(8,128)}) custom-call(s32[256]{0:T(256)} %refs_0_.3, s32[256]{0:T(256)} %refs_1_.3, s32[1]{0:T(128)S(6)} %copy.13.refs_2_, bf16[256,128,128]{2,1,0:T(8,128)(2,1)} %refs_3_.3, bf16[16,64,128]{2,1,0:T(8,128)(2,1)} %get-tuple-element.26.refs_4_, bf16[256,16,128]{2,1,0:T(8,128)(2,1)} %shard_map.91.refs_5_, ...), custom_call_target="tpu_custom_call" | custom-call | tf_op jit(solution)/shard_map/pallas_call | solution.py:335
  226.5 19.1 %shard_map.93.refs_1_ = f32[64,128]{1,0:T(8,128)} custom-call(f32[64,128]{1,0:T(8,128)} %get-tuple-element.30.x_ref), custom_call_target="tpu_custom_call" | custom-call | tf_op jit(solution)/shard_map/pallas_call | solution.py:97
  245.6 4.0 %shard_map.94 = (f32[16,64,128]{2,1,0:T(8,128)}, f32[32,128]{1,0:T(8,128)}) custom-call(f32[16,64,128]{2,1,0:T(8,128)} %get-tuple-element.29.refs_0_, f32[64,128]{1,0:T(8,128)} %shard_map.93.refs_1_, f32[16,64,128]{2,1,0:T(8,128)} %get-tuple-element.21.refs_6_.refs_2_.q0_ref, f32[16,64,128]{2,1,0:T(8,128)} %get-tuple-element.28.refs_7_.refs_3_.q1_ref), custom_call_target="tpu_custom_call" | custom-call | tf_op jit(solution)/shard_map/pallas_call | solution.py:351
  249.6 16.3 %shard_map.95.g_ref = f32[32,128]{1,0:T(8,128)} custom-call(f32[32,128]{1,0:T(8,128)} %get-tuple-element.32.x_ref), custom_call_target="tpu_custom_call" | custom-call | tf_op jit(solution)/shard_map/pallas_call | solution.py:97
  266.0 9.0 %shard_map.96 = f32[16,64,128]{2,1,0:T(8,128)} custom-call(f32[16,64,128]{2,1,0:T(8,128)} %get-tuple-element.31.z_ref, f32[32,128]{1,0:T(8,128)} %shard_map.95.g_ref, f32[64,192]{1,0:T(8,128)} %bitcast.3, f32[16,64,128]{2,1,0:T(8,128)} %get-tuple-element.21.refs_6_.refs_2_.q0_ref, f32[16,64,128]{2,1,0:T(8,128)} %get-tuple-element.28.refs_7_.refs_3_.q1_ref), custom_call_target="tpu_custom_call" | custom-call | tf_op jit(solution)/shard_map/pallas_call | solution.py:375
  (2 shorter events, 0.0 us)

commit v2 on v1

--- a/solution.py
+++ b/solution.py
@@ -21,13 +21,14 @@
 SMEM = pl.BlockSpec(memory_space=pltpu.SMEM)
 
 
-def ar_kernel(x_ref, o_ref, pbuf, xybuf, zbuf, fin, ss, rs):
+def place():
     row = lax.axis_index("row")
     col = lax.axis_index("col")
-    core = lax.rem(row, 2)
-    z = row // 2
-    prow = row + 1 - 2 * core
-    half = x_ref.shape[0] // 2
+    return row, col, row + 1 - 2 * lax.rem(row, 2)
+
+
+def greet():
+    row, col, prow = place()
     bar = pltpu.get_barrier_semaphore()
     pl.semaphore_signal(bar, inc=1, device_id=(prow, col), device_id_type=MESH)
 
@@ -42,15 +43,39 @@
         return c
 
     lax.fori_loop(1, 8, greet_z, 0)
-    pl.semaphore_wait(bar, 23)
+
+
+def greeted():
+    pl.semaphore_wait(pltpu.get_barrier_semaphore(), 23)
+
+
+def sum_scratch(rows):
+    half = rows // 2
+    return [
+        pltpu.VMEM((rows, 128), F32),
+        pltpu.VMEM((half, 128), F32),
+        pltpu.VMEM((16, half, 128), F32),
+        pltpu.VMEM((8, half, 128), F32),
+        pltpu.VMEM((rows, 128), F32),
+        pltpu.SemaphoreType.DMA((4,)),
+        pltpu.SemaphoreType.DMA((4,)),
+    ]
+
+
+def total(scratch):
+    xbuf, pbuf, xybuf, zbuf, fin, ss, rs = scratch
+    row, col, prow = place()
+    core = lax.rem(row, 2)
+    z = row // 2
+    half = pbuf.shape[0]
     mine = pl.ds(pl.multiple_of(core * half, half), half)
     other = pl.ds(pl.multiple_of((1 - core) * half, half), half)
     cp = pltpu.make_async_remote_copy(
-        x_ref.at[other], pbuf, ss.at[0], rs.at[0], device_id=(prow, col), device_id_type=MESH
+        xbuf.at[other], pbuf, ss.at[0], rs.at[0], device_id=(prow, col), device_id_type=MESH
     )
     cp.start()
     cp.wait()
-    xybuf[col] = x_ref[mine, :] + pbuf[...]
+    xybuf[col] = xbuf[mine, :] + pbuf[...]
 
     def send_xy(i, c):
         pltpu.make_async_remote_copy(
@@ -88,63 +113,7 @@
     )
     cp.start()
     cp.wait()
-    o_ref[...] = fin[...]
-
-
-def allreduce(x):
-    rows = x.shape[0]
-    half = rows // 2
-    return pl.pallas_call(
-        ar_kernel,
-        out_shape=jax.ShapeDtypeStruct(x.shape, F32),
-        in_specs=[VMEM],
-        out_specs=VMEM,
-        scratch_shapes=[
-            pltpu.VMEM((half, 128), F32),
-            pltpu.VMEM((16, half, 128), F32),
-            pltpu.VMEM((8, half, 128), F32),
-            pltpu.VMEM((rows, 128), F32),
-            pltpu.SemaphoreType.DMA((4,)),
-            pltpu.SemaphoreType.DMA((4,)),
-        ],
-        compiler_params=pltpu.CompilerParams(collective_id=rows // 32, has_side_effects=True),
-    )(x)
-
-
-def ex_kernel(s_ref, o_ref, ss, rs, ls):
-    row = lax.axis_index("row")
-    col = lax.axis_index("col")
-    me = row * 16 + col
-    lc = pltpu.make_async_copy(s_ref.at[me], o_ref.at[me], ls)
-    lc.start()
-
-    def go(i, c):
-        r2 = lax.rem(row + lax.rem(i, 16), 16)
-        c2 = lax.rem(col + i // 16, 16)
-        pltpu.make_async_remote_copy(
-            s_ref.at[r2 * 16 + c2], o_ref.at[me], ss, rs, device_id=(r2, c2), device_id_type=MESH
-        ).start()
-        return c
-
-    lax.fori_loop(1, 256, go, 0)
-    w = pltpu.make_async_remote_copy(
-        s_ref.at[pl.ds(0, 255)], o_ref.at[pl.ds(0, 255)], ss, rs,
-        device_id=(row, lax.rem(col + 1, 16)), device_id_type=MESH,
-    )
-    w.wait_recv()
-    w.wait_send()
-    lc.wait()
-
-
-def exchange(x):
-    return pl.pallas_call(
-        ex_kernel,
-        out_shape=jax.ShapeDtypeStruct(x.shape, x.dtype),
-        in_specs=[VMEM],
-        out_specs=VMEM,
-        scratch_shapes=[pltpu.SemaphoreType.DMA] * 3,
-        compiler_params=pltpu.CompilerParams(has_side_effects=True),
-    )(x)
+    return fin[...]
 
 
 def nt(a, b):
@@ -212,20 +181,31 @@
     return out
 
 
-def gram_kernel(x_ref, o_ref):
-    x = wide(x_ref)
-    o_ref[...] = fold(nt(x, x))
-
-
-def ortho_kernel(z_ref, g_ref, l_ref, t_ref, q_ref, p_ref, s_ref, lhs):
-    m = inverse_factor(unfold(g_ref[...]) * (1.0 / NODES))
-    put_wide(q_ref, nn(m, wide(z_ref)))
+def send_halo(q_ref, l_ref, t_ref, h_ref, scratch):
+    lhs, out, ss, rs, ls = scratch
+    row, col, prow = place()
+    me = row * 16 + col
     for t in range(RT):
-        p_ref[t] = q_ref[t].astype(BF16)
         lhs[64 * (t // 2):64 * (t // 2) + 64, 128 * (t % 2):128 * (t % 2) + 128] = q_ref[t].astype(BF16)
     node = lax.broadcasted_iota(jnp.int32, (256, 256), 0)
 
-    def chunk(c, carry):
+    def target(i):
+        return lax.rem(row + 8 + 5 * (i // 2), 16), lax.rem(i, 2) * 8
+
+    def send(i):
+        r2, c2 = target(i)
+        for u in range(8):
+            there = r2 * 16 + c2 + u
+
+            @pl.when(there != me)
+            def _():
+                pltpu.make_async_remote_copy(
+                    out.at[there], h_ref.at[me], ss, rs, device_id=(r2, c2 + u), device_id_type=MESH
+                ).start()
+
+    def chunk(i, carry):
+        r2, c2 = target(i)
+        c = 2 * r2 + c2 // 8
         lsel = jnp.concatenate([l_ref[pl.ds(2 * c, 1), :], l_ref[pl.ds(2 * c + 1, 1), :]], axis=1)
         tsel = jnp.concatenate([t_ref[pl.ds(2 * c, 1), :], t_ref[pl.ds(2 * c + 1, 1), :]], axis=1)
         hot = jnp.where(node == lsel, 1.0, 0.0).astype(BF16)
@@ -236,10 +216,84 @@
         for h in range(2):
             msgs = swap_groups([acc[16 * g:16 * g + 16, 128 * h:128 * h + 128] for g in range(4)])
             for q in range(4):
-                s_ref[8 * c + 4 * h + q] = msgs[q].astype(BF16)
+                out[8 * c + 4 * h + q] = msgs[q].astype(BF16)
+
+        @pl.when(i > 0)
+        def _():
+            send(i - 1)
+
         return carry
 
     lax.fori_loop(0, 32, chunk, 0)
+    send(31)
+    own = pltpu.make_async_copy(out.at[me], h_ref.at[me], ls)
+    own.start()
+    w = pltpu.make_async_remote_copy(
+        out.at[pl.ds(0, 255)], h_ref.at[pl.ds(0, 255)], ss, rs,
+        device_id=(prow, col), device_id_type=MESH,
+    )
+    w.wait_recv()
+    w.wait_send()
+    own.wait()
+
+
+def halo_scratch():
+    return [
+        pltpu.VMEM((512, 256), BF16),
+        pltpu.VMEM((DEVS, 16, 128), BF16),
+        pltpu.SemaphoreType.DMA,
+        pltpu.SemaphoreType.DMA,
+        pltpu.SemaphoreType.DMA,
+    ]
+
+
+def normalize(z, total_gram, q_ref, p_ref):
+    m = inverse_factor(unfold(total_gram) * (1.0 / NODES))
+    put_wide(q_ref, nn(m, z))
+    p_ref[...] = q_ref[...].astype(BF16)
+
+
+def first_kernel(x_ref, l_ref, t_ref, q_ref, p_ref, h_ref, *scratch):
+    greet()
+    x = wide(x_ref)
+    scratch[0][...] = fold(nt(x, x))
+    greeted()
+    g = total(scratch[:7])
+    normalize(wide(x_ref), g, q_ref, p_ref)
+    send_halo(q_ref, l_ref, t_ref, h_ref, scratch[7:])
+
+
+def residual(nb, y_ref, basis, c, z_ref):
+    z = wide(y_ref)
+    for i, b in enumerate(basis):
+        z = z - nn(unfold(c[32 * i:32 * i + 32]) * (1.0 / NODES), wide(b))
+    put_wide(z_ref, z)
+    return fold(nt(z, z))
+
+
+def next_kernel(y_ref, c_ref, q0_ref, l_ref, t_ref, q_ref, p_ref, h_ref, z_ref, *scratch):
+    greet()
+    scratch[0][...] = c_ref[...]
+    greeted()
+    c = total(scratch[:7])
+    scratch[7][...] = residual(1, y_ref, [q0_ref], c, z_ref)
+    g = total(scratch[7:14])
+    normalize(wide(z_ref), g, q_ref, p_ref)
+    send_halo(q_ref, l_ref, t_ref, h_ref, scratch[14:])
+
+
+def last_kernel(y_ref, c_ref, q0_ref, q1_ref, rot_ref, o_ref, z_ref, *scratch):
+    greet()
+    scratch[0][...] = c_ref[...]
+    rot = rot_ref[...]
+    greeted()
+    c = total(scratch[:7])
+    scratch[7][...] = residual(2, y_ref, [q0_ref, q1_ref], c, z_ref)
+    g = total(scratch[7:14])
+    m = inverse_factor(unfold(g) * (1.0 / NODES))
+    tail = nn(rot[:, 128:192], m)
+    o = nn(rot[:, 0:64], wide(q0_ref)) + nn(rot[:, 64:128], wide(q1_ref)) + nn(tail, wide(z_ref))
+    put_wide(o_ref, o)
 
 
 def apply_kernel(nb, *refs):
@@ -291,43 +345,19 @@
     c_ref[...] = jnp.concatenate([fold(nt(y, wide(b))) for b in basis], axis=0)
 
 
-def project_kernel(nb, *refs):
-    y_ref, c_ref = refs[:2]
-    basis = refs[2:2 + nb]
-    z_ref, g_ref = refs[2 + nb:]
-    z = wide(y_ref)
-    for i, b in enumerate(basis):
-        z = z - nn(unfold(c_ref[32 * i:32 * i + 32]) * (1.0 / NODES), wide(b))
-    put_wide(z_ref, z)
-    g_ref[...] = fold(nt(z, z))
-
-
-def final_kernel(z_ref, g_ref, rot_ref, q0_ref, q1_ref, o_ref):
-    m = inverse_factor(unfold(g_ref[...]) * (1.0 / NODES))
-    rot = rot_ref[...]
-    tail = nn(rot[:, 128:192], m)
-    o = nn(rot[:, 0:64], wide(q0_ref)) + nn(rot[:, 64:128], wide(q1_ref)) + nn(tail, wide(z_ref))
-    put_wide(o_ref, o)
-
-
 def block(dtype):
     return jax.ShapeDtypeStruct((RT, BLK, TILE), dtype)
 
 
-def gram(x):
+def remote(kernel, cid, outs, scratch, *operands):
     return pl.pallas_call(
-        gram_kernel, out_shape=jax.ShapeDtypeStruct((32, 128), F32), in_specs=[VMEM], out_specs=VMEM
-    )(x)
-
-
-def ortho(z, g, lsel, tsel):
-    return pl.pallas_call(
-        ortho_kernel,
-        out_shape=(block(F32), block(BF16), jax.ShapeDtypeStruct((DEVS, 16, 128), BF16)),
-        in_specs=[VMEM] * 4,
-        out_specs=(VMEM,) * 3,
-        scratch_shapes=[pltpu.VMEM((512, 256), BF16)],
-    )(z, g, lsel, tsel)
+        kernel,
+        out_shape=outs,
+        in_specs=[VMEM] * len(operands),
+        out_specs=(VMEM,) * len(outs),
+        scratch_shapes=scratch,
+        compiler_params=pltpu.CompilerParams(collective_id=cid, has_side_effects=True),
+    )(*operands)
 
 
 def apply_graph(rows, cols, count, values, p, halo, basis):
@@ -346,35 +376,22 @@
     )(rows, cols, count, values, p, halo, *basis)
 
 
-def project(y, c, basis):
-    nb = len(basis)
-    return pl.pallas_call(
-        functools.partial(project_kernel, nb),
-        out_shape=(block(F32), jax.ShapeDtypeStruct((32, 128), F32)),
-        in_specs=[VMEM] * (2 + nb),
-        out_specs=(VMEM,) * 2,
-    )(y, c, *basis)
-
-
 def body(start, values, rows, cols, count, send_rows, send_count, rotation):
     slot = jnp.arange(32, dtype=jnp.int32)
     wanted = send_rows[0]
     lsel = (wanted % 256).reshape(64, 128)
     tsel = jnp.where(slot[None, :] < send_count[0][:, None], wanted // 256, -1).reshape(64, 128)
-    g = allreduce(gram(start))
-    q, p, out = ortho(start, g, lsel, tsel)
-    basis = [q]
-    for k in range(2):
-        halo = exchange(out)
-        y, c = apply_graph(rows, cols, count, values, p, halo, basis)
-        z, g = project(y, allreduce(c), basis)
-        g = allreduce(g)
-        if k == 0:
-            q, p, out = ortho(z, g, lsel, tsel)
-            basis.append(q)
-    return pl.pallas_call(
-        final_kernel, out_shape=block(F32), in_specs=[VMEM] * 5, out_specs=VMEM
-    )(z, g, rotation.T, basis[0], basis[1])
+    state = (block(F32), block(BF16), jax.ShapeDtypeStruct((DEVS, 16, 128), BF16))
+    held = [pltpu.VMEM((RT, BLK, TILE), F32)]
+    q0, p, halo = remote(first_kernel, 1, state, sum_scratch(32) + halo_scratch(), start, lsel, tsel)
+    y, c = apply_graph(rows, cols, count, values, p, halo, [q0])
+    q1, p, halo = remote(
+        next_kernel, 2, state, held + sum_scratch(32) + sum_scratch(32) + halo_scratch(), y, c, q0, lsel, tsel
+    )
+    y, c = apply_graph(rows, cols, count, values, p, halo, [q0, q1])
+    return remote(
+        last_kernel, 3, (block(F32),), held + sum_scratch(64) + sum_scratch(32), y, c, q0, q1, rotation.T
+    )[0]
 
 
 def solution(mesh):

time: 277 us -> 216 us (0.78)
  Pallas kernels: 270 us -> 209 us
    pallas_call x13 -> x3, Pallas kernels: 231 us -> 180 us  [remote(): pl.pallas_call(kernel, out_shape=outs, in_specs=[VMEM] * len(operands), o...]
    pallas_call x2, Pallas kernels: 39.7 us -> 29.3 us  [apply_graph(): pl.pallas_call(functools.partial(apply_kernel, nb), out_shape=(block(F32)...]
where the time goes in v2:
time: 216 us
  Pallas kernels  209 us (97%)
  local copies, waits for them, and re-layouts  3.71 us (2%)
    pallas_call x3, Pallas kernels, remote(): pl.pallas_call(kernel, out_shape=outs, in_specs=[VMEM] * len(operands), o...  180 us
    pallas_call x2, Pallas kernels, apply_graph(): pl.pallas_call(functools.partial(apply_kernel, nb), out_shape=(block(F32)...  29.3 us

profile of v2, /device:TPU:1, one launch (start us, length us, event | category | flops | bytes accessed | tf_op | source)
XLA Modules:
  0.0 215.7 jit_solution(288028573103441079)
XLA Ops:
  0.7 0.5 broadcast.32
  1.2 1.3 reduce.3
  2.5 0.1 lt.30
  2.6 0.1 lt.32
  2.7 0.1 copy.11
  2.8 0.1 copy.12
  2.9 0.9 copy.10
  3.7 0.1 squeeze.3
  3.8 0.7 fusion
  4.5 58.3 %shard_map.82 = (f32[16,64,128]{2,1,0:T(8,128)}, bf16[16,64,128]{2,1,0:T(8,128)(2,1)}, bf16[256,16,128]{2,1,0:T(8,128)(2,1)}) custom-call(f32[16,64,128]{2,1,0:T(8,128)} %x_ref.1, s32[64,128]{1,0:T(8,128)} %get-tuple-element.26.l_ref, s32[64,128]{1,0:T(8,128)} %get-tuple-element.25.t_ref), custom_call_target="tpu_custom_call" | custom-call | tf_op jit(solution)/shard_map/pallas_call | solution.py:353
  62.8 14.3 %shard_map.83 = (f32[16,64,128]{2,1,0:T(8,128)}, f32[32,128]{1,0:T(8,128)}) custom-call(s32[256]{0:T(256)} %refs_0_.3, s32[256]{0:T(256)} %refs_1_.3, s32[1]{0:T(128)S(6)} %copy.14.refs_2_, bf16[256,128,128]{2,1,0:T(8,128)(2,1)} %refs_3_.3, bf16[16,64,128]{2,1,0:T(8,128)(2,1)} %get-tuple-element.15.refs_4_, bf16[256,16,128]{2,1,0:T(8,128)(2,1)} %get-tuple-element.16.refs_5_, ...), custom_call_target="tpu_custom_call" | custom-call | tf_op jit(solution)/shard_map/pallas_call | solution.py:365
  77.1 72.4 %shard_map.84 = (f32[16,64,128]{2,1,0:T(8,128)}, bf16[16,64,128]{2,1,0:T(8,128)(2,1)}, bf16[256,16,128]{2,1,0:T(8,128)(2,1)}) custom-call(f32[16,64,128]{2,1,0:T(8,128)} %get-tuple-element.18.y_ref, f32[32,128]{1,0:T(8,128)} %get-tuple-element.19.c_ref, f32[16,64,128]{2,1,0:T(8,128)} %get-tuple-element.17.refs_6_.q0_ref, s32[64,128]{1,0:T(8,128)} %get-tuple-element.26.l_ref, ...), custom_call_target="tpu_custom_call" | custom-call | tf_op jit(solution)/shard_map/pallas_call | solution.py:353
  149.4 15.0 %shard_map.85 = (f32[16,64,128]{2,1,0:T(8,128)}, f32[64,128]{1,0:T(8,128)}) custom-call(s32[256]{0:T(256)} %refs_0_.3, s32[256]{0:T(256)} %refs_1_.3, s32[1]{0:T(128)S(6)} %copy.14.refs_2_, bf16[256,128,128]{2,1,0:T(8,128)(2,1)} %refs_3_.3, bf16[16,64,128]{2,1,0:T(8,128)(2,1)} %get-tuple-element.20.refs_4_, bf16[256,16,128]{2,1,0:T(8,128)(2,1)} %get-tuple-element.21.refs_5_, ...), custom_call_target="tpu_custom_call" | custom-call | tf_op jit(solution)/shard_map/pallas_call | solution.py:365
  164.4 49.3 %shard_map.86 = f32[16,64,128]{2,1,0:T(8,128)} custom-call(f32[16,64,128]{2,1,0:T(8,128)} %get-tuple-element.23.y_ref, f32[64,128]{1,0:T(8,128)} %get-tuple-element.24.c_ref, f32[16,64,128]{2,1,0:T(8,128)} %get-tuple-element.17.refs_6_.q0_ref, f32[16,64,128]{2,1,0:T(8,128)} %get-tuple-element.22.refs_7_.q1_ref, f32[64,192]{1,0:T(8,128)} %bitcast.3), custom_call_target="tpu_custom_call" | custom-call | tf_op jit(solution)/shard_map/pallas_call | solution.py:353
  213.8 1.9 copy.15
  (2 shorter events, 0.0 us)

commit v3 on v2

--- a/solution.py
+++ b/solution.py
@@ -148,15 +148,21 @@
     blocks = [
         jnp.where(lane == sub + (64 + 8 * b), 1.0, wide_g[8 * b:8 * b + 8]) for b in range(8)
     ]
-    for j in range(64):
+    for j in range(0, 64, 2):
         jb, jr = divmod(j, 8)
-        pivot_row = blocks[jb][jr:jr + 1, :]
-        scaled = pivot_row / pivot_row[:, j:j + 1]
+        c1 = [jnp.broadcast_to(blocks[b][:, j:j + 1], (8, 128)) for b in range(jb, 8)]
+        c2 = [jnp.broadcast_to(blocks[b][:, j + 1:j + 2], (8, 128)) for b in range(jb, 8)]
+        r1 = blocks[jb][jr:jr + 1, :]
+        ia = 1.0 / c1[0][jr:jr + 1, :]
+        ratio = c1[0][jr + 1:jr + 2, :] * ia
+        r2 = blocks[jb][jr + 1:jr + 2, :] - ratio * r1
+        w2 = r2 / (c2[0][jr + 1:jr + 2, :] - ratio * c1[0][jr + 1:jr + 2, :])
+        w1 = r1 * ia - ratio * w2
         for b in range(jb, 8):
-            c = blocks[b][:, j:j + 1]
+            new = blocks[b] - (c1[b - jb] * w1 + c2[b - jb] * w2)
             if b == jb:
-                c = jnp.where(sub[:, :1] > jr, c, 0.0)
-            blocks[b] = blocks[b] - c * scaled
+                new = jnp.where(sub > jr + 1, new, jnp.where(sub == jr + 1, r2, blocks[b]))
+            blocks[b] = new
     out = []
     for b in range(8):
         d = jnp.sum(jnp.where(lane == sub + 8 * b, blocks[b], 0.0), axis=1, keepdims=True)
@@ -164,59 +170,59 @@
     return jnp.concatenate(out, axis=0)
 
 
-def swap_groups(parts):
-    lane = lax.broadcasted_iota(jnp.int32, (16, 128), 1)
-    low = lane < 64
-    even = lax.rem(lane, 64) < 32
-    first = {}
-    for g in range(2):
-        a, b = parts[g], parts[g + 2]
-        first[0, g] = jnp.where(low, a, pltpu.roll(b, 64, 1))
-        first[1, g] = jnp.where(low, pltpu.roll(a, 64, 1), b)
-    out = []
-    for h in range(2):
-        a, b = first[h, 0], first[h, 1]
-        out.append(jnp.where(even, a, pltpu.roll(b, 32, 1)))
-        out.append(jnp.where(even, pltpu.roll(a, 96, 1), b))
-    return out
+def swap_matrix():
+    k = lax.broadcasted_iota(jnp.int32, (512, 512), 0)
+    n = lax.broadcasted_iota(jnp.int32, (512, 512), 1)
+    goal = lax.rem(k // 32, 4) * 128 + (k // 128) * 32 + lax.rem(k, 32)
+    return jnp.where(goal == n, 1.0, 0.0).astype(BF16)
 
 
 def send_halo(q_ref, l_ref, t_ref, h_ref, scratch):
-    lhs, out, ss, rs, ls = scratch
+    lhs, swap, out, ss, rs, ls = scratch
     row, col, prow = place()
     me = row * 16 + col
     for t in range(RT):
         lhs[64 * (t // 2):64 * (t // 2) + 64, 128 * (t % 2):128 * (t % 2) + 128] = q_ref[t].astype(BF16)
     node = lax.broadcasted_iota(jnp.int32, (256, 256), 0)
 
-    def target(i):
-        return lax.rem(row + 8 + 5 * (i // 2), 16), lax.rem(i, 2) * 8
+    def target(i, h):
+        return lax.rem(row + 8 + 5 * (2 * i + h), 16)
 
     def send(i):
-        r2, c2 = target(i)
-        for u in range(8):
-            there = r2 * 16 + c2 + u
-
-            @pl.when(there != me)
-            def _():
-                pltpu.make_async_remote_copy(
-                    out.at[there], h_ref.at[me], ss, rs, device_id=(r2, c2 + u), device_id_type=MESH
-                ).start()
+        for h in range(2):
+            r2 = target(i, h)
+            for u in range(16):
+                there = r2 * 16 + u
+
+                @pl.when(there != me)
+                def _():
+                    pltpu.make_async_remote_copy(
+                        out.at[there], h_ref.at[me], ss, rs, device_id=(r2, u), device_id_type=MESH
+                    ).start()
 
     def chunk(i, carry):
-        r2, c2 = target(i)
-        c = 2 * r2 + c2 // 8
-        lsel = jnp.concatenate([l_ref[pl.ds(2 * c, 1), :], l_ref[pl.ds(2 * c + 1, 1), :]], axis=1)
-        tsel = jnp.concatenate([t_ref[pl.ds(2 * c, 1), :], t_ref[pl.ds(2 * c + 1, 1), :]], axis=1)
-        hot = jnp.where(node == lsel, 1.0, 0.0).astype(BF16)
-        r = jnp.dot(lhs[...], hot, preferred_element_type=F32)
-        acc = jnp.zeros((64, 256), F32)
-        for t in range(8):
-            acc = acc + jnp.where(tsel == t, r[64 * t:64 * t + 64], 0.0)
+        parts = []
+        for e in range(4):
+            c = 4 * target(i, e // 2) + 2 * (e % 2)
+            lsel = jnp.concatenate([l_ref[pl.ds(c, 1), :], l_ref[pl.ds(c + 1, 1), :]], axis=1)
+            tsel = jnp.concatenate([t_ref[pl.ds(c, 1), :], t_ref[pl.ds(c + 1, 1), :]], axis=1)
+            hot = jnp.where(node == lsel, 1.0, 0.0).astype(BF16)
+            r = jnp.dot(lhs[...], hot, preferred_element_type=F32)
+            acc = jnp.zeros((64, 256), F32)
+            for t in range(8):
+                acc = acc + jnp.where(tsel == t, r[64 * t:64 * t + 64], 0.0)
+            acc = acc.astype(BF16)
+            for h in range(2):
+                parts.append(
+                    jnp.concatenate([acc[16 * g:16 * g + 16, 128 * h:128 * h + 128] for g in range(4)], axis=1)
+                )
+        msgs = jnp.dot(jnp.concatenate(parts, axis=0), swap[...], preferred_element_type=F32).astype(BF16)
         for h in range(2):
-            msgs = swap_groups([acc[16 * g:16 * g + 16, 128 * h:128 * h + 128] for g in range(4)])
-            for q in range(4):
-                out[8 * c + 4 * h + q] = msgs[q].astype(BF16)
+            first = 16 * target(i, h)
+            for v in range(4):
+                for q in range(4):
+                    u = 4 * h + v
+                    out[first + 4 * v + q] = msgs[16 * u:16 * u + 16, 128 * q:128 * q + 128]
 
         @pl.when(i > 0)
         def _():
@@ -224,8 +230,8 @@
 
         return carry
 
-    lax.fori_loop(0, 32, chunk, 0)
-    send(31)
+    lax.fori_loop(0, 8, chunk, 0)
+    send(7)
     own = pltpu.make_async_copy(out.at[me], h_ref.at[me], ls)
     own.start()
     w = pltpu.make_async_remote_copy(
@@ -240,6 +246,7 @@
 def halo_scratch():
     return [
         pltpu.VMEM((512, 256), BF16),
+        pltpu.VMEM((512, 512), BF16),
         pltpu.VMEM((DEVS, 16, 128), BF16),
         pltpu.SemaphoreType.DMA,
         pltpu.SemaphoreType.DMA,
@@ -257,6 +264,7 @@
     greet()
     x = wide(x_ref)
     scratch[0][...] = fold(nt(x, x))
+    scratch[8][...] = swap_matrix()
     greeted()
     g = total(scratch[:7])
     normalize(wide(x_ref), g, q_ref, p_ref)
@@ -274,6 +282,7 @@
 def next_kernel(y_ref, c_ref, q0_ref, l_ref, t_ref, q_ref, p_ref, h_ref, z_ref, *scratch):
     greet()
     scratch[0][...] = c_ref[...]
+    scratch[15][...] = swap_matrix()
     greeted()
     c = total(scratch[:7])
     scratch[7][...] = residual(1, y_ref, [q0_ref], c, z_ref)
@@ -299,43 +308,42 @@
 def apply_kernel(nb, *refs):
     rows, cols, count, values, p_ref, h_ref = refs[:6]
     basis = refs[6:6 + nb]
-    y_ref, c_ref, src, acc, buf, sem = refs[6 + nb:]
+    y_ref, c_ref, src, acc, swap, buf, sem = refs[6 + nb:]
     n = count[0]
     nchunk = (n + CHUNK - 1) // CHUNK
 
     def fetch(c):
-        slot = lax.rem(c, 3)
-        return pltpu.make_async_copy(values.at[pl.ds(c * CHUNK, CHUNK)], buf.at[slot], sem.at[slot])
-
-    fetch(0).start()
-
-    @pl.when(nchunk > 1)
-    def _():
-        fetch(1).start()
-
+        part = pl.ds(c * CHUNK, CHUNK)
+        return pltpu.make_async_copy(values.at[part], buf.at[part], sem.at[c])
+
+    def begin(c, carry):
+        fetch(c).start()
+        return carry
+
+    lax.fori_loop(0, nchunk, begin, 0)
     acc[...] = jnp.zeros_like(acc)
     src[0:RT] = p_ref[...]
-
-    def unpack(h, c):
-        parts = swap_groups([h_ref[4 * h + q].astype(F32) for q in range(4)])
-        for g in range(4):
-            src[RT + h, 16 * g:16 * g + 16, :] = parts[g].astype(BF16)
-        return c
-
-    lax.fori_loop(0, 64, unpack, 0)
+    swap[...] = swap_matrix()
+
+    def unpack(h, carry):
+        parts = [
+            jnp.concatenate([h_ref[32 * h + 4 * u + q] for q in range(4)], axis=1) for u in range(8)
+        ]
+        tiles = jnp.dot(jnp.concatenate(parts, axis=0), swap[...], preferred_element_type=F32).astype(BF16)
+        for u in range(8):
+            for g in range(4):
+                src[RT + 8 * h + u, 16 * g:16 * g + 16, :] = tiles[16 * u:16 * u + 16, 128 * g:128 * g + 128]
+        return carry
+
+    lax.fori_loop(0, 8, unpack, 0)
 
     def step(c, carry):
-        @pl.when(c + 2 < nchunk)
-        def _():
-            fetch(c + 2).start()
-
         fetch(c).wait()
-        slot = lax.rem(c, 3)
         for u in range(CHUNK):
             k = c * CHUNK + u
             r = jnp.where(k < n, rows[k], RT)
             acc[r] += lax.dot_general(
-                src[cols[k]], buf[slot, u], (((1,), (1,)), ((), ())), preferred_element_type=F32
+                src[cols[k]], buf[k], (((1,), (1,)), ((), ())), preferred_element_type=F32
             )
         return carry
 
@@ -370,8 +378,9 @@
         scratch_shapes=[
             pltpu.VMEM((80, BLK, TILE), BF16),
             pltpu.VMEM((RT + 1, BLK, TILE), F32),
-            pltpu.VMEM((3, CHUNK, TILE, TILE), BF16),
-            pltpu.SemaphoreType.DMA((3,)),
+            pltpu.VMEM((512, 512), BF16),
+            pltpu.VMEM((DEVS, TILE, TILE), BF16),
+            pltpu.SemaphoreType.DMA((DEVS // CHUNK,)),
         ],
     )(rows, cols, count, values, p, halo, *basis)
 

time: 216 us -> 194 us (0.90)
  Pallas kernels: 209 us -> 187 us
    pallas_call x2, Pallas kernels: 29.3 us -> 13.7 us  [apply_graph(): pl.pallas_call(functools.partial(apply_kernel, nb), out_shape=(block(F32)...]
    pallas_call x3, Pallas kernels: 180 us -> 173 us  [remote(): pl.pallas_call(kernel, out_shape=outs, in_specs=[VMEM] * len(operands), o...]
where the time goes in v3:
time: 194 us; the launch traced here: 193 us
  Pallas kernels  187 us (96%)
  local copies, waits for them, and re-layouts  3.71 us (2%)
  other arithmetic  2 us (1%)
    pallas_call x3, Pallas kernels, remote(): pl.pallas_call(kernel, out_shape=outs, in_specs=[VMEM] * len(operands), o...  173 us
    pallas_call x2, Pallas kernels, apply_graph(): pl.pallas_call(functools.partial(apply_kernel, nb), out_shape=(block(F32)...  13.7 us

profile of v3, /device:TPU:1, one launch (start us, length us, event | category | flops | bytes accessed | tf_op | source)
XLA Modules:
  0.0 193.3 jit_solution(6862934475568203771)
XLA Ops:
  0.7 0.5 broadcast.32
  1.2 1.3 reduce.3
  2.5 0.1 lt.30
  2.6 0.1 lt.32
  2.7 0.1 copy.11
  2.8 0.1 copy.12
  2.9 0.9 copy.10
  3.7 0.1 squeeze.3
  3.8 0.7 fusion
  4.5 56.8 %shard_map.82 = (f32[16,64,128]{2,1,0:T(8,128)}, bf16[16,64,128]{2,1,0:T(8,128)(2,1)}, bf16[256,16,128]{2,1,0:T(8,128)(2,1)}) custom-call(f32[16,64,128]{2,1,0:T(8,128)} %x_ref.1, s32[64,128]{1,0:T(8,128)} %get-tuple-element.26.l_ref, s32[64,128]{1,0:T(8,128)} %get-tuple-element.25.t_ref), custom_call_target="tpu_custom_call" | custom-call | tf_op jit(solution)/shard_map/pallas_call | solution.py:361
  61.3 6.5 %shard_map.83 = (f32[16,64,128]{2,1,0:T(8,128)}, f32[32,128]{1,0:T(8,128)}) custom-call(s32[256]{0:T(256)} %refs_0_.3, s32[256]{0:T(256)} %refs_1_.3, s32[1]{0:T(128)S(6)} %copy.14.refs_2_, bf16[256,128,128]{2,1,0:T(8,128)(2,1)} %refs_3_.3, bf16[16,64,128]{2,1,0:T(8,128)(2,1)} %get-tuple-element.15.refs_4_, bf16[256,16,128]{2,1,0:T(8,128)(2,1)} %get-tuple-element.16.refs_5_, ...), custom_call_target="tpu_custom_call" | custom-call | tf_op jit(solution)/shard_map/pallas_call | solution.py:373
  67.8 70.0 %shard_map.84 = (f32[16,64,128]{2,1,0:T(8,128)}, bf16[16,64,128]{2,1,0:T(8,128)(2,1)}, bf16[256,16,128]{2,1,0:T(8,128)(2,1)}) custom-call(f32[16,64,128]{2,1,0:T(8,128)} %get-tuple-element.18.y_ref, f32[32,128]{1,0:T(8,128)} %get-tuple-element.19.c_ref, f32[16,64,128]{2,1,0:T(8,128)} %get-tuple-element.17.refs_6_.q0_ref, s32[64,128]{1,0:T(8,128)} %get-tuple-element.26.l_ref, ...), custom_call_target="tpu_custom_call" | custom-call | tf_op jit(solution)/shard_map/pallas_call | solution.py:361
  137.8 7.2 %shard_map.85 = (f32[16,64,128]{2,1,0:T(8,128)}, f32[64,128]{1,0:T(8,128)}) custom-call(s32[256]{0:T(256)} %refs_0_.3, s32[256]{0:T(256)} %refs_1_.3, s32[1]{0:T(128)S(6)} %copy.14.refs_2_, bf16[256,128,128]{2,1,0:T(8,128)(2,1)} %refs_3_.3, bf16[16,64,128]{2,1,0:T(8,128)(2,1)} %get-tuple-element.20.refs_4_, bf16[256,16,128]{2,1,0:T(8,128)(2,1)} %get-tuple-element.21.refs_5_, ...), custom_call_target="tpu_custom_call" | custom-call | tf_op jit(solution)/shard_map/pallas_call | solution.py:373
  145.0 46.4 %shard_map.86 = f32[16,64,128]{2,1,0:T(8,128)} custom-call(f32[16,64,128]{2,1,0:T(8,128)} %get-tuple-element.23.y_ref, f32[64,128]{1,0:T(8,128)} %get-tuple-element.24.c_ref, f32[16,64,128]{2,1,0:T(8,128)} %get-tuple-element.17.refs_6_.q0_ref, f32[16,64,128]{2,1,0:T(8,128)} %get-tuple-element.22.refs_7_.q1_ref, f32[64,192]{1,0:T(8,128)} %bitcast.3), custom_call_target="tpu_custom_call" | custom-call | tf_op jit(solution)/shard_map/pallas_call | solution.py:361
  191.4 1.9 copy.15
  (2 shorter events, 0.0 us)

commit v4 on v3

--- a/solution.py
+++ b/solution.py
@@ -185,25 +185,32 @@
         lhs[64 * (t // 2):64 * (t // 2) + 64, 128 * (t % 2):128 * (t % 2) + 128] = q_ref[t].astype(BF16)
     node = lax.broadcasted_iota(jnp.int32, (256, 256), 0)
 
-    def target(i, h):
-        return lax.rem(row + 8 + 5 * (2 * i + h), 16)
+    core = lax.rem(row, 2)
+
+    def target(i):
+        k = i // 2
+        away = (k + 1) // 2
+        dz = jnp.where(lax.rem(k, 2) == 1, 4 - away, 4 + away)
+        flip = lax.rem(i, 2)
+        return 2 * lax.rem(row // 2 + dz, 8) + core + flip - 2 * core * flip
 
     def send(i):
-        for h in range(2):
-            r2 = target(i, h)
-            for u in range(16):
-                there = r2 * 16 + u
-
-                @pl.when(there != me)
-                def _():
-                    pltpu.make_async_remote_copy(
-                        out.at[there], h_ref.at[me], ss, rs, device_id=(r2, u), device_id_type=MESH
-                    ).start()
+        r2 = target(i)
+        for u in range(16):
+            c2 = lax.rem(col + 10 + u, 16)
+            there = r2 * 16 + c2
+
+            @pl.when(there != me)
+            def _():
+                pltpu.make_async_remote_copy(
+                    out.at[there], h_ref.at[me], ss, rs, device_id=(r2, c2), device_id_type=MESH
+                ).start()
 
     def chunk(i, carry):
         parts = []
-        for e in range(4):
-            c = 4 * target(i, e // 2) + 2 * (e % 2)
+        r2 = target(i)
+        for e in range(2):
+            c = 4 * r2 + 2 * e
             lsel = jnp.concatenate([l_ref[pl.ds(c, 1), :], l_ref[pl.ds(c + 1, 1), :]], axis=1)
             tsel = jnp.concatenate([t_ref[pl.ds(c, 1), :], t_ref[pl.ds(c + 1, 1), :]], axis=1)
             hot = jnp.where(node == lsel, 1.0, 0.0).astype(BF16)
@@ -217,12 +224,9 @@
                     jnp.concatenate([acc[16 * g:16 * g + 16, 128 * h:128 * h + 128] for g in range(4)], axis=1)
                 )
         msgs = jnp.dot(jnp.concatenate(parts, axis=0), swap[...], preferred_element_type=F32).astype(BF16)
-        for h in range(2):
-            first = 16 * target(i, h)
-            for v in range(4):
-                for q in range(4):
-                    u = 4 * h + v
-                    out[first + 4 * v + q] = msgs[16 * u:16 * u + 16, 128 * q:128 * q + 128]
+        for v in range(4):
+            for q in range(4):
+                out[16 * r2 + 4 * v + q] = msgs[16 * v:16 * v + 16, 128 * q:128 * q + 128]
 
         @pl.when(i > 0)
         def _():
@@ -230,8 +234,8 @@
 
         return carry
 
-    lax.fori_loop(0, 8, chunk, 0)
-    send(7)
+    lax.fori_loop(0, 16, chunk, 0)
+    send(15)
     own = pltpu.make_async_copy(out.at[me], h_ref.at[me], ls)
     own.start()
     w = pltpu.make_async_remote_copy(
@@ -260,11 +264,26 @@
     p_ref[...] = q_ref[...].astype(BF16)
 
 
-def first_kernel(x_ref, l_ref, t_ref, q_ref, p_ref, h_ref, *scratch):
+def index_tables(w_ref, n_ref, l_ref, t_ref):
+    wanted = jnp.concatenate([w_ref[pl.ds(q, 64, stride=4), :] for q in range(4)], axis=1)
+    dest = lax.broadcasted_iota(jnp.int32, (64, 256), 1)
+    group = lax.broadcasted_iota(jnp.int32, (64, 256), 0)
+    spread = jnp.where(dest // 4 == group, n_ref[...].astype(F32), 0.0).astype(BF16)
+    dest = lax.broadcasted_iota(jnp.int32, (256, 128), 0)
+    lane = lax.broadcasted_iota(jnp.int32, (256, 128), 1)
+    pick = jnp.where(lax.rem(dest, 4) == lane // 32, 1.0, 0.0).astype(BF16)
+    live = jnp.dot(spread, pick, preferred_element_type=F32)
+    slot = lax.rem(lax.broadcasted_iota(jnp.int32, (64, 128), 1), 32)
+    l_ref[...] = lax.rem(wanted, 256)
+    t_ref[...] = jnp.where(slot.astype(F32) < live, wanted // 256, -1)
+
+
+def first_kernel(x_ref, w_ref, n_ref, q_ref, p_ref, h_ref, l_ref, t_ref, *scratch):
     greet()
     x = wide(x_ref)
     scratch[0][...] = fold(nt(x, x))
     scratch[8][...] = swap_matrix()
+    index_tables(w_ref, n_ref, l_ref, t_ref)
     greeted()
     g = total(scratch[:7])
     normalize(wide(x_ref), g, q_ref, p_ref)
@@ -364,7 +383,9 @@
         in_specs=[VMEM] * len(operands),
         out_specs=(VMEM,) * len(outs),
         scratch_shapes=scratch,
-        compiler_params=pltpu.CompilerParams(collective_id=cid, has_side_effects=True),
+        compiler_params=pltpu.CompilerParams(
+            collective_id=cid, has_side_effects=True, vmem_limit_bytes=24 * 1024 * 1024
+        ),
     )(*operands)
 
 
@@ -373,7 +394,7 @@
     return pl.pallas_call(
         functools.partial(apply_kernel, nb),
         out_shape=(block(F32), jax.ShapeDtypeStruct((32 * nb, 128), F32)),
-        in_specs=[SMEM] * 3 + [pl.BlockSpec(memory_space=pl.ANY)] + [VMEM] * (2 + nb),
+        in_specs=[SMEM] * 3 + [pl.BlockSpec(memory_space=pltpu.HBM)] + [VMEM] * (2 + nb),
         out_specs=(VMEM,) * 2,
         scratch_shapes=[
             pltpu.VMEM((80, BLK, TILE), BF16),
@@ -382,17 +403,17 @@
             pltpu.VMEM((DEVS, TILE, TILE), BF16),
             pltpu.SemaphoreType.DMA((DEVS // CHUNK,)),
         ],
+        compiler_params=pltpu.CompilerParams(vmem_limit_bytes=24 * 1024 * 1024),
     )(rows, cols, count, values, p, halo, *basis)
 
 
 def body(start, values, rows, cols, count, send_rows, send_count, rotation):
-    slot = jnp.arange(32, dtype=jnp.int32)
-    wanted = send_rows[0]
-    lsel = (wanted % 256).reshape(64, 128)
-    tsel = jnp.where(slot[None, :] < send_count[0][:, None], wanted // 256, -1).reshape(64, 128)
     state = (block(F32), block(BF16), jax.ShapeDtypeStruct((DEVS, 16, 128), BF16))
     held = [pltpu.VMEM((RT, BLK, TILE), F32)]
-    q0, p, halo = remote(first_kernel, 1, state, sum_scratch(32) + halo_scratch(), start, lsel, tsel)
+    table = jax.ShapeDtypeStruct((64, 128), jnp.int32)
+    q0, p, halo, lsel, tsel = remote(
+        first_kernel, 1, state + (table, table), sum_scratch(32) + halo_scratch(), start, send_rows[0], send_count
+    )
     y, c = apply_graph(rows, cols, count, values, p, halo, [q0])
     q1, p, halo = remote(
         next_kernel, 2, state, held + sum_scratch(32) + sum_scratch(32) + halo_scratch(), y, c, q0, lsel, tsel

time: 194 us -> 188 us (0.969)
  Pallas kernels: 187 us -> 179 us
  local copies, waits for them, and re-layouts: 3.71 us -> 8.11 us
  other arithmetic: 2 us -> 0 us
    pallas_call x3, Pallas kernels: 173 us -> 167 us  [remote(): pl.pallas_call(kernel, out_shape=outs, in_specs=[VMEM] * len(operands), o...]
    unnamed x3 -> x16, local copies, waits for them, and re-layouts: 3.28 us -> 8.11 us
    pallas_call x2, Pallas kernels: 13.7 us -> 11.6 us  [apply_graph(): pl.pallas_call(functools.partial(apply_kernel, nb), out_shape=(block(F32)...]
where the time goes in v4:
time: 188 us
  Pallas kernels  179 us (95%)
  local copies, waits for them, and re-layouts  8.11 us (4%)
    pallas_call x3, Pallas kernels, remote(): pl.pallas_call(kernel, out_shape=outs, in_specs=[VMEM] * len(operands), o...  167 us
    pallas_call x2, Pallas kernels, apply_graph(): pl.pallas_call(functools.partial(apply_kernel, nb), out_shape=(block(F32)...  11.6 us
    unnamed x16, local copies, waits for them, and re-layouts  8.11 us

profile of v4, /device:TPU:1, one launch (start us, length us, event | category | flops | bytes accessed | tf_op | source)
XLA Modules:
  0.0 187.9 jit_solution(1892762035219547253)
XLA Ops:
  0.7 0.9 copy.9
  1.5 0.0 copy-start.2
  1.5 1.0 copy-done.2
  2.6 0.0 copy-start.6
  2.6 0.7 copy-done.6
  3.2 55.6 %shard_map.82 = (f32[16,64,128]{2,1,0:T(8,128)S(1)}, bf16[16,64,128]{2,1,0:T(8,128)(2,1)S(1)}, bf16[256,16,128]{2,1,0:T(8,128)(2,1)S(1)}, s32[64,128]{1,0:T(8,128)S(1)}, s32[64,128]{1,0:T(8,128)S(1)}) custom-call(f32[16,64,128]{2,1,0:T(8,128)S(1)} %copy-done.2, s32[256,32]{1,0:T(8,128)S(1)} %bitcast.2, s32[1,256]{1,0:T(1,128)S(1)} %copy-done.6), custom_call_target="tpu_custom_call" | custom-call | tf_op jit(solution)/shard_map/pallas_call | solution.py:380
  58.8 0.0 copy-start
  58.8 3.4 %copy-done = bf16[256,128,128]{2,1,0:T(8,128)(2,1)S(1)} copy-done((bf16[256,128,128]{2,1,0:T(8,128)(2,1)S(1)}, bf16[256,128,128]{2,1,0:T(8,128)(2,1)}, u32[]{:S(2)}) %copy-start) | copy-done | bytes 8388632
  62.2 0.0 copy-start.4
  62.2 0.7 copy-done.4
  62.9 0.0 copy-start.5
  62.9 0.7 copy-done.5
  63.5 0.0 copy-start.1
  63.5 5.5 %shard_map.83 = (f32[16,64,128]{2,1,0:T(8,128)S(1)}, f32[32,128]{1,0:T(8,128)S(1)}) custom-call(s32[256]{0:T(256)S(1)} %copy-done.4, s32[256]{0:T(256)S(1)} %copy-done.5, s32[1]{0:T(128)S(6)} %copy.11.refs_2_, bf16[256,128,128]{2,1,0:T(8,128)(2,1)S(1)} %copy-done, bf16[16,64,128]{2,1,0:T(8,128)(2,1)S(1)} %get-tuple-element.17.refs_4_, ...), custom_call_target="tpu_custom_call" | custom-call | tf_op jit(solution)/shard_map/pallas_call | solution.py:394
  69.1 0.0 copy-start.3
  69.1 67.3 %shard_map.84 = (f32[16,64,128]{2,1,0:T(8,128)S(1)}, bf16[16,64,128]{2,1,0:T(8,128)(2,1)S(1)}, bf16[256,16,128]{2,1,0:T(8,128)(2,1)S(1)}) custom-call(f32[16,64,128]{2,1,0:T(8,128)S(1)} %get-tuple-element.20.y_ref, f32[32,128]{1,0:T(8,128)S(1)} %get-tuple-element.21.c_ref, f32[16,64,128]{2,1,0:T(8,128)S(1)} %get-tuple-element.19.refs_6_.q0_ref, ...), custom_call_target="tpu_custom_call" | custom-call | tf_op jit(solution)/shard_map/pallas_call | solution.py:380
  136.4 0.0 copy-done.1
  136.4 6.1 %shard_map.85 = (f32[16,64,128]{2,1,0:T(8,128)S(1)}, f32[64,128]{1,0:T(8,128)S(1)}) custom-call(s32[256]{0:T(256)S(1)} %copy-done.4, s32[256]{0:T(256)S(1)} %copy-done.5, s32[1]{0:T(128)S(6)} %copy.11.refs_2_, bf16[256,128,128]{2,1,0:T(8,128)(2,1)S(1)} %copy-done.1, bf16[16,64,128]{2,1,0:T(8,128)(2,1)S(1)} %get-tuple-element.24.refs_4_, ...), custom_call_target="tpu_custom_call" | custom-call | tf_op jit(solution)/shard_map/pallas_call | solution.py:394
  142.5 0.0 copy-done.3
  142.5 44.5 %shard_map.86 = f32[16,64,128]{2,1,0:T(8,128)S(1)} custom-call(f32[16,64,128]{2,1,0:T(8,128)S(1)} %get-tuple-element.27.y_ref, f32[64,128]{1,0:T(8,128)S(1)} %get-tuple-element.28.c_ref, f32[16,64,128]{2,1,0:T(8,128)S(1)} %get-tuple-element.19.refs_6_.q0_ref, f32[16,64,128]{2,1,0:T(8,128)S(1)} %get-tuple-element.26.refs_7_.q1_ref, f32[64,192]{1,0:T(8,128)S(1)} %bitcast.3), custom_call_target="tpu_custom_call" | custom-call | tf_op jit(solution)/shard_map/pallas_call | solution.py:380
  187.1 0.8 copy.12
Async XLA Ops:
  1.5 1.0 copy-start.2
  2.6 0.7 copy-start.6
  58.8 3.4 %copy-start = (bf16[256,128,128]{2,1,0:T(8,128)(2,1)S(1)}, bf16[256,128,128]{2,1,0:T(8,128)(2,1)}, u32[]{:S(2)}) copy-start(bf16[256,128,128]{2,1,0:T(8,128)(2,1)} %refs_3_.3) | copy-start | bytes 25165828
  62.2 0.7 copy-start.4
  62.9 0.7 copy-start.5
  63.5 72.9 %copy-start.1 = (bf16[256,128,128]{2,1,0:T(8,128)(2,1)S(1)}, bf16[256,128,128]{2,1,0:T(8,128)(2,1)}, u32[]{:S(2)}) copy-start(bf16[256,128,128]{2,1,0:T(8,128)(2,1)} %refs_3_.3) | copy-start | bytes 25165828
  69.1 73.5 %copy-start.3 = (f32[192,64]{0,1:T(8,128)S(1)}, f32[192,64]{0,1:T(8,128)}, u32[]{:S(2)}) copy-start(f32[192,64]{0,1:T(8,128)} %param.15) | copy-start | bytes 147460

commit v5 on v4

--- a/solution.py
+++ b/solution.py
@@ -62,7 +62,7 @@
     ]
 
 
-def total(scratch):
+def total(scratch, during=None):
     xbuf, pbuf, xybuf, zbuf, fin, ss, rs = scratch
     row, col, prow = place()
     core = lax.rem(row, 2)
@@ -85,6 +85,8 @@
         return c
 
     lax.fori_loop(1, 16, send_xy, 0)
+    if during is not None:
+        during()
     w = pltpu.make_async_remote_copy(
         xybuf.at[pl.ds(0, 15)], xybuf.at[pl.ds(0, 15)], ss.at[1], rs.at[1],
         device_id=(prow, col), device_id_type=MESH,
@@ -282,10 +284,13 @@
     greet()
     x = wide(x_ref)
     scratch[0][...] = fold(nt(x, x))
-    scratch[8][...] = swap_matrix()
-    index_tables(w_ref, n_ref, l_ref, t_ref)
     greeted()
-    g = total(scratch[:7])
+
+    def during():
+        scratch[8][...] = swap_matrix()
+        index_tables(w_ref, n_ref, l_ref, t_ref)
+
+    g = total(scratch[:7], during)
     normalize(wide(x_ref), g, q_ref, p_ref)
     send_halo(q_ref, l_ref, t_ref, h_ref, scratch[7:])
 
@@ -301,9 +306,12 @@
 def next_kernel(y_ref, c_ref, q0_ref, l_ref, t_ref, q_ref, p_ref, h_ref, z_ref, *scratch):
     greet()
     scratch[0][...] = c_ref[...]
-    scratch[15][...] = swap_matrix()
     greeted()
-    c = total(scratch[:7])
+
+    def during():
+        scratch[15][...] = swap_matrix()
+
+    c = total(scratch[:7], during)
     scratch[7][...] = residual(1, y_ref, [q0_ref], c, z_ref)
     g = total(scratch[7:14])
     normalize(wide(z_ref), g, q_ref, p_ref)
@@ -315,31 +323,25 @@
     scratch[0][...] = c_ref[...]
     rot = rot_ref[...]
     greeted()
-    c = total(scratch[:7])
+
+    def during():
+        put_wide(o_ref, nn(rot[:, 0:64], wide(q0_ref)) + nn(rot[:, 64:128], wide(q1_ref)))
+
+    c = total(scratch[:7], during)
     scratch[7][...] = residual(2, y_ref, [q0_ref, q1_ref], c, z_ref)
     g = total(scratch[7:14])
     m = inverse_factor(unfold(g) * (1.0 / NODES))
     tail = nn(rot[:, 128:192], m)
-    o = nn(rot[:, 0:64], wide(q0_ref)) + nn(rot[:, 64:128], wide(q1_ref)) + nn(tail, wide(z_ref))
-    put_wide(o_ref, o)
+    put_wide(o_ref, wide(o_ref) + nn(tail, wide(z_ref)))
 
 
 def apply_kernel(nb, *refs):
     rows, cols, count, values, p_ref, h_ref = refs[:6]
     basis = refs[6:6 + nb]
-    y_ref, c_ref, src, acc, swap, buf, sem = refs[6 + nb:]
+    y_ref, c_ref, src, acc, swap = refs[6 + nb:]
     n = count[0]
     nchunk = (n + CHUNK - 1) // CHUNK
 
-    def fetch(c):
-        part = pl.ds(c * CHUNK, CHUNK)
-        return pltpu.make_async_copy(values.at[part], buf.at[part], sem.at[c])
-
-    def begin(c, carry):
-        fetch(c).start()
-        return carry
-
-    lax.fori_loop(0, nchunk, begin, 0)
     acc[...] = jnp.zeros_like(acc)
     src[0:RT] = p_ref[...]
     swap[...] = swap_matrix()
@@ -357,12 +359,11 @@
     lax.fori_loop(0, 8, unpack, 0)
 
     def step(c, carry):
-        fetch(c).wait()
         for u in range(CHUNK):
             k = c * CHUNK + u
             r = jnp.where(k < n, rows[k], RT)
             acc[r] += lax.dot_general(
-                src[cols[k]], buf[k], (((1,), (1,)), ((), ())), preferred_element_type=F32
+                src[cols[k]], values[k], (((1,), (1,)), ((), ())), preferred_element_type=F32
             )
         return carry
 
@@ -383,6 +384,7 @@
         in_specs=[VMEM] * len(operands),
         out_specs=(VMEM,) * len(outs),
         scratch_shapes=scratch,
+        cost_estimate=pl.CostEstimate(flops=20_000_000_000, bytes_accessed=100_000_000, transcendentals=0),
         compiler_params=pltpu.CompilerParams(
             collective_id=cid, has_side_effects=True, vmem_limit_bytes=24 * 1024 * 1024
         ),
@@ -394,14 +396,12 @@
     return pl.pallas_call(
         functools.partial(apply_kernel, nb),
         out_shape=(block(F32), jax.ShapeDtypeStruct((32 * nb, 128), F32)),
-        in_specs=[SMEM] * 3 + [pl.BlockSpec(memory_space=pltpu.HBM)] + [VMEM] * (2 + nb),
+        in_specs=[SMEM] * 3 + [VMEM] * (3 + nb),
         out_specs=(VMEM,) * 2,
         scratch_shapes=[
             pltpu.VMEM((80, BLK, TILE), BF16),
             pltpu.VMEM((RT + 1, BLK, TILE), F32),
             pltpu.VMEM((512, 512), BF16),
-            pltpu.VMEM((DEVS, TILE, TILE), BF16),
-            pltpu.SemaphoreType.DMA((DEVS // CHUNK,)),
         ],
         compiler_params=pltpu.CompilerParams(vmem_limit_bytes=24 * 1024 * 1024),
     )(rows, cols, count, values, p, halo, *basis)

time: 188 us -> 180 us (0.957)
  local copies, waits for them, and re-layouts: 8.11 us -> 3.38 us
  Pallas kernels: 179 us -> 176 us
    pallas_call x3, Pallas kernels: 167 us -> 160 us  [remote(): pl.pallas_call(kernel, out_shape=outs, in_specs=[VMEM] * len(operands), o...]
    pallas_call x2, Pallas kernels: 11.6 us -> 16.6 us  [apply_graph(): pl.pallas_call(functools.partial(apply_kernel, nb), out_shape=(block(F32)...]
    unnamed x16 -> x14, local copies, waits for them, and re-layouts: 8.11 us -> 3.38 us
where the time goes in v5:
time: 180 us
  Pallas kernels  176 us (98%)
  local copies, waits for them, and re-layouts  3.38 us (2%)
    pallas_call x3, Pallas kernels, remote(): pl.pallas_call(kernel, out_shape=outs, in_specs=[VMEM] * len(operands), o...  160 us
    pallas_call x2, Pallas kernels, apply_graph(): pl.pallas_call(functools.partial(apply_kernel, nb), out_shape=(block(F32)...  16.6 us

profile of v5, /device:TPU:1, one launch (start us, length us, event | category | flops | bytes accessed | tf_op | source)
XLA Modules:
  0.0 180.3 jit_solution(2025379250358138283)
XLA Ops:
  0.7 0.9 copy.9
  1.5 0.0 copy-start.3
  1.5 1.0 copy-done.3
  2.6 0.0 copy-start.5
  2.6 0.7 copy-done.5
  3.2 0.0 copy-start
  3.2 0.0 copy-start.1
  3.2 0.0 copy-start.2
  3.2 55.7 %shard_map.82 = (f32[16,64,128]{2,1,0:T(8,128)S(1)}, bf16[16,64,128]{2,1,0:T(8,128)(2,1)S(1)}, bf16[256,16,128]{2,1,0:T(8,128)(2,1)S(1)}, s32[64,128]{1,0:T(8,128)S(1)}, s32[64,128]{1,0:T(8,128)S(1)}) custom-call(f32[16,64,128]{2,1,0:T(8,128)S(1)} %copy-done.3, s32[256,32]{1,0:T(8,128)S(1)} %bitcast.2, s32[1,256]{1,0:T(1,128)S(1)} %copy-done.5), custom_call_target="tpu_custom_call" | custom-call | flops 20000000000 | bytes 100000000 | tf_op jit(solution)/shard_map/pallas_call | solution.py:381
  58.9 0.0 copy-done
  58.9 0.0 copy-done.1
  59.0 0.0 copy-done.2
  59.0 8.0 %shard_map.83 = (f32[16,64,128]{2,1,0:T(8,128)S(1)}, f32[32,128]{1,0:T(8,128)S(1)}) custom-call(s32[256]{0:T(256)S(1)} %copy-done.1, s32[256]{0:T(256)S(1)} %copy-done.2, s32[1]{0:T(128)S(6)} %copy.11.refs_2_, bf16[256,128,128]{2,1,0:T(8,128)(2,1)S(1)} %copy-done, bf16[16,64,128]{2,1,0:T(8,128)(2,1)S(1)} %get-tuple-element.17.refs_4_, ...), custom_call_target="tpu_custom_call" | custom-call | tf_op jit(solution)/shard_map/pallas_call | solution.py:396
  67.0 64.6 %shard_map.84 = (f32[16,64,128]{2,1,0:T(8,128)S(1)}, bf16[16,64,128]{2,1,0:T(8,128)(2,1)S(1)}, bf16[256,16,128]{2,1,0:T(8,128)(2,1)S(1)}) custom-call(f32[16,64,128]{2,1,0:T(8,128)S(1)} %get-tuple-element.20.y_ref, f32[32,128]{1,0:T(8,128)S(1)} %get-tuple-element.21.c_ref, f32[16,64,128]{2,1,0:T(8,128)S(1)} %get-tuple-element.19.refs_6_.q0_ref, ...), custom_call_target="tpu_custom_call" | custom-call | flops 20000000000 | bytes 100000000 | tf_op jit(solution)/shard_map/pallas_call | solution.py:381
  131.5 0.0 copy-start.4
  131.5 8.6 %shard_map.85 = (f32[16,64,128]{2,1,0:T(8,128)S(1)}, f32[64,128]{1,0:T(8,128)S(1)}) custom-call(s32[256]{0:T(256)S(1)} %copy-done.1, s32[256]{0:T(256)S(1)} %copy-done.2, s32[1]{0:T(128)S(6)} %copy.11.refs_2_, bf16[256,128,128]{2,1,0:T(8,128)(2,1)S(1)} %copy-done, bf16[16,64,128]{2,1,0:T(8,128)(2,1)S(1)} %get-tuple-element.24.refs_4_, ...), custom_call_target="tpu_custom_call" | custom-call | tf_op jit(solution)/shard_map/pallas_call | solution.py:396
  140.1 0.0 copy-done.4
  140.1 39.4 %shard_map.86 = f32[16,64,128]{2,1,0:T(8,128)S(1)} custom-call(f32[16,64,128]{2,1,0:T(8,128)S(1)} %get-tuple-element.27.y_ref, f32[64,128]{1,0:T(8,128)S(1)} %get-tuple-element.28.c_ref, f32[16,64,128]{2,1,0:T(8,128)S(1)} %get-tuple-element.19.refs_6_.q0_ref, f32[16,64,128]{2,1,0:T(8,128)S(1)} %get-tuple-element.26.refs_7_.q1_ref, f32[64,192]{1,0:T(8,128)S(1)} %bitcast.3), custom_call_target="tpu_custom_call" | custom-call | flops 20000000000 | bytes 100000000 | tf_op jit(solution)/shard_map/pallas_call | solution.py:381
  179.5 0.8 copy.12
Async XLA Ops:
  1.5 1.0 copy-start.3
  2.6 0.7 copy-start.5
  3.2 55.7 %copy-start = (bf16[256,128,128]{2,1,0:T(8,128)(2,1)S(1)}, bf16[256,128,128]{2,1,0:T(8,128)(2,1)}, u32[]{:S(2)}) copy-start(bf16[256,128,128]{2,1,0:T(8,128)(2,1)} %refs_3_.3) | copy-start | bytes 25165828
  3.2 55.7 %copy-start.1 = (s32[256]{0:T(256)S(1)}, s32[256]{0:T(256)}, u32[]{:S(2)}) copy-start(s32[256]{0:T(256)} %refs_0_.3) | copy-start | bytes 3076
  3.2 55.7 %copy-start.2 = (s32[256]{0:T(256)S(1)}, s32[256]{0:T(256)}, u32[]{:S(2)}) copy-start(s32[256]{0:T(256)} %refs_1_.3) | copy-start | bytes 3076
  131.5 8.6 %copy-start.4 = (f32[192,64]{0,1:T(8,128)S(1)}, f32[192,64]{0,1:T(8,128)}, u32[]{:S(2)}) copy-start(f32[192,64]{0,1:T(8,128)} %param.15) | copy-start | bytes 147460

commit v6 on v5

--- a/solution.py
+++ b/solution.py
@@ -47,6 +47,33 @@
 
 def greeted():
     pl.semaphore_wait(pltpu.get_barrier_semaphore(), 23)
+
+
+def greet_all():
+    row, col, _ = place()
+    bar = pltpu.get_barrier_semaphore()
+
+    def one(i, c):
+        pl.semaphore_signal(bar, inc=1, device_id=(row, lax.rem(col + i, 16)), device_id_type=MESH)
+        pl.semaphore_signal(bar, inc=1, device_id=(lax.rem(row + i, 16), col), device_id_type=MESH)
+        return c
+
+    lax.fori_loop(1, 16, one, 0)
+
+
+def greeted_all_first(sem):
+    row, col, _ = place()
+    pl.semaphore_wait(pltpu.get_barrier_semaphore(), 30)
+
+    def one(i, c):
+        pl.semaphore_signal(sem, inc=1, device_id=(lax.rem(row + i, 16), col), device_id_type=MESH)
+        return c
+
+    lax.fori_loop(1, 16, one, 0)
+
+
+def greeted_all_second(sem):
+    pl.semaphore_wait(sem, 15)
 
 
 def sum_scratch(rows):
@@ -179,7 +206,7 @@
     return jnp.where(goal == n, 1.0, 0.0).astype(BF16)
 
 
-def send_halo(q_ref, l_ref, t_ref, h_ref, scratch):
+def send_halo(q_ref, l_ref, t_ref, h_ref, scratch, ready=None):
     lhs, swap, out, ss, rs, ls = scratch
     row, col, prow = place()
     me = row * 16 + col
@@ -236,6 +263,8 @@
 
         return carry
 
+    if ready is not None:
+        ready()
     lax.fori_loop(0, 16, chunk, 0)
     send(15)
     own = pltpu.make_async_copy(out.at[me], h_ref.at[me], ls)
@@ -295,44 +324,69 @@
     send_halo(q_ref, l_ref, t_ref, h_ref, scratch[7:])
 
 
-def residual(nb, y_ref, basis, c, z_ref):
-    z = wide(y_ref)
-    for i, b in enumerate(basis):
-        z = z - nn(unfold(c[32 * i:32 * i + 32]) * (1.0 / NODES), wide(b))
-    put_wide(z_ref, z)
-    return fold(nt(z, z))
-
-
-def next_kernel(y_ref, c_ref, q0_ref, l_ref, t_ref, q_ref, p_ref, h_ref, z_ref, *scratch):
+def diagonal(g):
+    i = lax.broadcasted_iota(jnp.int32, (BLK, BLK), 0)
+    j = lax.broadcasted_iota(jnp.int32, (BLK, BLK), 1)
+    return jnp.sum(jnp.where(i == j, g, 0.0), axis=1, keepdims=True)
+
+
+def project_kernel(nb, *refs):
+    y_ref, c_ref = refs[:2]
+    basis = refs[2:2 + nb]
+    z_ref, g_ref, ok_ref = refs[2 + nb:5 + nb]
+    scratch = refs[5 + nb:]
     greet()
     scratch[0][...] = c_ref[...]
     greeted()
-
-    def during():
-        scratch[15][...] = swap_matrix()
-
-    c = total(scratch[:7], during)
-    scratch[7][...] = residual(1, y_ref, [q0_ref], c, z_ref)
-    g = total(scratch[7:14])
+    c = total(scratch) * (1.0 / NODES)
+    whole = unfold(c[32 * nb:])
+    g = whole
+    z = wide(y_ref)
+    for i, b in enumerate(basis):
+        part = unfold(c[32 * i:32 * i + 32])
+        g = g - nt(part, part)
+        z = z - nn(part, wide(b))
+    put_wide(z_ref, z)
+    g_ref[...] = fold(g)
+    kept = jnp.min(diagonal(g) - 0.25 * diagonal(whole), axis=0, keepdims=True)
+    ok_ref[...] = jnp.broadcast_to(jnp.where(kept > 0.0, 1, 0), (8, 128))
+
+
+def fast_kernel(z_ref, g_ref, l_ref, t_ref, q_ref, p_ref, h_ref, sem, *scratch):
+    greet_all()
+    m = inverse_factor(unfold(g_ref[...]))
+    scratch[1][...] = swap_matrix()
+    greeted_all_first(sem)
+    put_wide(q_ref, nn(m, wide(z_ref)))
+    p_ref[...] = q_ref[...].astype(BF16)
+    send_halo(q_ref, l_ref, t_ref, h_ref, scratch, lambda: greeted_all_second(sem))
+
+
+def slow_kernel(z_ref, g_ref, l_ref, t_ref, q_ref, p_ref, h_ref, *scratch):
+    greet()
+    z = wide(z_ref)
+    scratch[0][...] = fold(nt(z, z))
+    scratch[8][...] = swap_matrix()
+    greeted()
+    g = total(scratch[:7])
     normalize(wide(z_ref), g, q_ref, p_ref)
-    send_halo(q_ref, l_ref, t_ref, h_ref, scratch[14:])
-
-
-def last_kernel(y_ref, c_ref, q0_ref, q1_ref, rot_ref, o_ref, z_ref, *scratch):
+    send_halo(q_ref, l_ref, t_ref, h_ref, scratch[7:])
+
+
+def gram_kernel(z_ref, g_ref, o_ref, *scratch):
     greet()
-    scratch[0][...] = c_ref[...]
+    z = wide(z_ref)
+    scratch[0][...] = fold(nt(z, z))
+    greeted()
+    o_ref[...] = total(scratch) * (1.0 / NODES)
+
+
+def last_kernel(z_ref, g_ref, q0_ref, q1_ref, rot_ref, o_ref):
     rot = rot_ref[...]
-    greeted()
-
-    def during():
-        put_wide(o_ref, nn(rot[:, 0:64], wide(q0_ref)) + nn(rot[:, 64:128], wide(q1_ref)))
-
-    c = total(scratch[:7], during)
-    scratch[7][...] = residual(2, y_ref, [q0_ref, q1_ref], c, z_ref)
-    g = total(scratch[7:14])
-    m = inverse_factor(unfold(g) * (1.0 / NODES))
+    m = inverse_factor(unfold(g_ref[...]))
     tail = nn(rot[:, 128:192], m)
-    put_wide(o_ref, wide(o_ref) + nn(tail, wide(z_ref)))
+    o = nn(rot[:, 0:64], wide(q0_ref)) + nn(rot[:, 64:128], wide(q1_ref)) + nn(tail, wide(z_ref))
+    put_wide(o_ref, o)
 
 
 def apply_kernel(nb, *refs):
@@ -370,7 +424,7 @@
     lax.fori_loop(0, nchunk, step, 0)
     y_ref[...] = acc[0:RT]
     y = wide(acc)
-    c_ref[...] = jnp.concatenate([fold(nt(y, wide(b))) for b in basis], axis=0)
+    c_ref[...] = jnp.concatenate([fold(nt(y, wide(b))) for b in basis] + [fold(nt(y, y))], axis=0)
 
 
 def block(dtype):
@@ -395,7 +449,7 @@
     nb = len(basis)
     return pl.pallas_call(
         functools.partial(apply_kernel, nb),
-        out_shape=(block(F32), jax.ShapeDtypeStruct((32 * nb, 128), F32)),
+        out_shape=(block(F32), jax.ShapeDtypeStruct((32 * nb + 32, 128), F32)),
         in_specs=[SMEM] * 3 + [VMEM] * (3 + nb),
         out_specs=(VMEM,) * 2,
         scratch_shapes=[
@@ -409,19 +463,39 @@
 
 def body(start, values, rows, cols, count, send_rows, send_count, rotation):
     state = (block(F32), block(BF16), jax.ShapeDtypeStruct((DEVS, 16, 128), BF16))
-    held = [pltpu.VMEM((RT, BLK, TILE), F32)]
     table = jax.ShapeDtypeStruct((64, 128), jnp.int32)
     q0, p, halo, lsel, tsel = remote(
         first_kernel, 1, state + (table, table), sum_scratch(32) + halo_scratch(), start, send_rows[0], send_count
     )
     y, c = apply_graph(rows, cols, count, values, p, halo, [q0])
-    q1, p, halo = remote(
-        next_kernel, 2, state, held + sum_scratch(32) + sum_scratch(32) + halo_scratch(), y, c, q0, lsel, tsel
-    )
+    z, g, ok = project(2, y, c, [q0])
+
+    def fast(z, g, l, t):
+        return tuple(remote(fast_kernel, 3, state, [pltpu.SemaphoreType.REGULAR] + halo_scratch(), z, g, l, t))
+
+    def slow(z, g, l, t):
+        return tuple(remote(slow_kernel, 4, state, sum_scratch(32) + halo_scratch(), z, g, l, t))
+
+    q1, p, halo = lax.cond(ok[0, 0] > 0, fast, slow, z, g, lsel, tsel)
     y, c = apply_graph(rows, cols, count, values, p, halo, [q0, q1])
-    return remote(
-        last_kernel, 3, (block(F32),), held + sum_scratch(64) + sum_scratch(32), y, c, q0, q1, rotation.T
-    )[0]
+    z, g, ok = project(5, y, c, [q0, q1])
+    small = (jax.ShapeDtypeStruct((32, 128), F32),)
+    g = lax.cond(
+        ok[0, 0] > 0, lambda z, g: g, lambda z, g: remote(gram_kernel, 6, small, sum_scratch(32), z, g)[0], z, g
+    )
+    return pl.pallas_call(
+        last_kernel,
+        out_shape=block(F32),
+        in_specs=[VMEM] * 5,
+        out_specs=VMEM,
+        compiler_params=pltpu.CompilerParams(vmem_limit_bytes=24 * 1024 * 1024),
+    )(z, g, q0, q1, rotation.T)
+
+
+def project(cid, y, c, basis):
+    nb = len(basis)
+    outs = (block(F32), jax.ShapeDtypeStruct((32, 128), F32), jax.ShapeDtypeStruct((8, 128), jnp.int32))
+    return remote(functools.partial(project_kernel, nb), cid, outs, sum_scratch(32 * nb + 32), y, c, *basis)
 
 
 def solution(mesh):

time: 180 us -> 168 us (0.933)
  Pallas kernels: 176 us -> 157 us
  local copies, waits for them, and re-layouts: 3.38 us -> 7.8 us
    pallas_call x3 -> x4, Pallas kernels: 160 us -> 141 us  [remote(): pl.pallas_call(kernel, out_shape=outs, in_specs=[VMEM] * len(operands), o...]
    pallas_call x2, Pallas kernels: 16.6 us -> 10.8 us  [apply_graph(): pl.pallas_call(functools.partial(apply_kernel, nb), out_shape=(block(F32)...]
    pallas_call x0 -> x1, Pallas kernels: none -> 5.76 us  [body(): pl.pallas_call(last_kernel, out_shape=block(F32), in_specs=[VMEM] * 5, ou...]
    unnamed x14 -> x15, local copies, waits for them, and re-layouts: 3.38 us -> 6.77 us
where the time goes in v6:
time: 168 us; the launch traced here: 167 us
  Pallas kernels  157 us (93%)
  local copies, waits for them, and re-layouts  7.8 us (5%)
  between operations  2.06 us (1%)
    pallas_call x4, Pallas kernels, remote(): pl.pallas_call(kernel, out_shape=outs, in_specs=[VMEM] * len(operands), o...  141 us
    pallas_call x2, Pallas kernels, apply_graph(): pl.pallas_call(functools.partial(apply_kernel, nb), out_shape=(block(F32)...  10.8 us
    unnamed x15, local copies, waits for them, and re-layouts  6.77 us
    pallas_call x1, Pallas kernels, body(): pl.pallas_call(last_kernel, out_shape=block(F32), in_specs=[VMEM] * 5, ou...  5.76 us

profile of v6, /device:TPU:1, one launch (start us, length us, event | category | flops | bytes accessed | tf_op | source)
XLA Modules:
  0.0 167.0 jit_solution(13552035876661086253)
XLA Ops:
  0.7 0.9 copy.9
  1.5 0.0 copy-start.5
  1.5 1.0 copy-done.5
  2.6 0.0 copy-start.6
  2.6 0.7 copy-done.6
  3.2 0.0 copy-start
  3.2 0.0 copy-start.3
  3.2 0.0 copy-start.4
  3.2 55.7 %shard_map.82 = (f32[16,64,128]{2,1,0:T(8,128)S(1)}, bf16[16,64,128]{2,1,0:T(8,128)(2,1)S(1)}, bf16[256,16,128]{2,1,0:T(8,128)(2,1)S(1)}, s32[64,128]{1,0:T(8,128)S(1)}, s32[64,128]{1,0:T(8,128)S(1)}) custom-call(f32[16,64,128]{2,1,0:T(8,128)S(1)} %copy-done.5, s32[256,32]{1,0:T(8,128)S(1)} %bitcast.4, s32[1,256]{1,0:T(1,128)S(1)} %copy-done.6), custom_call_target="tpu_custom_call" | custom-call | flops 20000000000 | bytes 100000000 | tf_op jit(solution)/shard_map/pallas_call | solution.py:435
  58.9 0.0 copy-done
  58.9 0.0 copy-done.3
  59.0 0.0 copy-done.4
  59.0 5.1 %shard_map.83 = (f32[16,64,128]{2,1,0:T(8,128)S(1)}, f32[64,128]{1,0:T(8,128)S(1)}) custom-call(s32[256]{0:T(256)S(1)} %copy-done.3, s32[256]{0:T(256)S(1)} %copy-done.4, s32[1]{0:T(128)S(6)} %copy.19.refs_2_, bf16[256,128,128]{2,1,0:T(8,128)(2,1)S(1)} %copy-done, bf16[16,64,128]{2,1,0:T(8,128)(2,1)S(1)} %get-tuple-element.57.refs_4_, ...), custom_call_target="tpu_custom_call" | custom-call | tf_op jit(solution)/shard_map/pallas_call | solution.py:450
  64.1 23.4 %shard_map.84 = (f32[16,64,128]{2,1,0:T(8,128)S(1)}, f32[32,128]{1,0:T(8,128)S(1)}, s32[8,128]{1,0:T(8,128)S(1)}) custom-call(f32[16,64,128]{2,1,0:T(8,128)S(1)} %get-tuple-element.60.refs_0_, f32[64,128]{1,0:T(8,128)S(1)} %get-tuple-element.61.refs_1_, f32[16,64,128]{2,1,0:T(8,128)S(1)} %get-tuple-element.59.refs_6_.refs_2_.q0_ref), custom_call_target="tpu_custom_call" | custom-call | flops 20000000000 | bytes 100000000 | tf_op jit(solution)/shard_map/pallas_call | solution.py:435
  87.4 0.5 slice.6
  88.6 36.2 %conditional.2 = ((f32[16,64,128]{2,1,0:T(8,128)S(1)}, bf16[16,64,128]{2,1,0:T(8,128)(2,1)S(1)}, bf16[256,16,128]{2,1,0:T(8,128)(2,1)S(1)})) conditional(s32[]{:T(128)} %bitcast.1, (f32[16,64,128]{2,1,0:T(8,128)S(1)}, f32[32,128]{1,0:T(8,128)S(1)}, s32[64,128]{1,0:T(8,128)S(1)}, s32[64,128]{1,0:T(8,128)S(1)}) %tuple.17, ...), branch_computations={%region_0.0_spmd, %region_1.0_spmd} | conditional | flops 20000000000 | bytes 100000008 | solution.py:479
  88.6 36.1 %branch_1_fun.1 = (f32[16,64,128]{2,1,0:T(8,128)S(1)}, bf16[16,64,128]{2,1,0:T(8,128)(2,1)S(1)}, bf16[256,16,128]{2,1,0:T(8,128)(2,1)S(1)}) custom-call(f32[16,64,128]{2,1,0:T(8,128)S(1)} %get-tuple-element.33.z_ref, f32[32,128]{1,0:T(8,128)S(1)} %get-tuple-element.34.g_ref, s32[64,128]{1,0:T(8,128)S(1)} %get-tuple-element.35.l_ref, ...), custom_call_target="tpu_custom_call" | custom-call | flops 20000000000 | bytes 100000000 | tf_op jit(solution)/shard_map/cond/branch_1_fun/pallas_call | solution.py:435
  124.8 0.0 copy-start.1
  124.8 3.4 %copy-done.1 = bf16[256,128,128]{2,1,0:T(8,128)(2,1)S(1)} copy-done((bf16[256,128,128]{2,1,0:T(8,128)(2,1)S(1)}, bf16[256,128,128]{2,1,0:T(8,128)(2,1)}, u32[]{:S(2)}) %copy-start.1) | copy-done | bytes 8388632
  128.2 5.7 %shard_map.85 = (f32[16,64,128]{2,1,0:T(8,128)S(1)}, f32[96,128]{1,0:T(8,128)S(1)}) custom-call(s32[256]{0:T(256)S(1)} %copy-done.3, s32[256]{0:T(256)S(1)} %copy-done.4, s32[1]{0:T(128)S(6)} %copy.19.refs_2_, bf16[256,128,128]{2,1,0:T(8,128)(2,1)S(1)} %copy-done.1, bf16[16,64,128]{2,1,0:T(8,128)(2,1)S(1)} %get-tuple-element.67.refs_4_, ...), custom_call_target="tpu_custom_call" | custom-call | tf_op jit(solution)/shard_map/pallas_call | solution.py:450
  133.9 25.4 %shard_map.86 = (f32[16,64,128]{2,1,0:T(8,128)S(1)}, f32[32,128]{1,0:T(8,128)S(1)}, s32[8,128]{1,0:T(8,128)S(1)}) custom-call(f32[16,64,128]{2,1,0:T(8,128)S(1)} %get-tuple-element.70.refs_0_, f32[96,128]{1,0:T(8,128)S(1)} %get-tuple-element.71.refs_1_, f32[16,64,128]{2,1,0:T(8,128)S(1)} %get-tuple-element.59.refs_6_.refs_2_.q0_ref, ...), custom_call_target="tpu_custom_call" | custom-call | flops 20000000000 | bytes 100000000 | tf_op jit(solution)/shard_map/pallas_call | solution.py:435
  159.2 0.5 slice.7
  160.4 0.0 copy-start.2
  160.4 0.8 copy-done.2
  161.3 5.8 %shard_map.87 = f32[16,64,128]{2,1,0:T(8,128)} custom-call(f32[16,64,128]{2,1,0:T(8,128)S(1)} %get-tuple-element.72.z_ref, f32[32,128]{1,0:T(8,128)S(1)} %get-tuple-element.82.g_ref, f32[16,64,128]{2,1,0:T(8,128)S(1)} %get-tuple-element.59.refs_6_.refs_2_.q0_ref, f32[16,64,128]{2,1,0:T(8,128)S(1)} %get-tuple-element.69.refs_7_.refs_3_.q1_ref, ...), custom_call_target="tpu_custom_call" | custom-call | tf_op jit(solution)/shard_map/pallas_call | solution.py:486
  (1 shorter events, 0.0 us)
Async XLA Ops:
  1.5 1.0 copy-start.5
  2.6 0.7 copy-start.6
  3.2 55.7 %copy-start = (bf16[256,128,128]{2,1,0:T(8,128)(2,1)S(1)}, bf16[256,128,128]{2,1,0:T(8,128)(2,1)}, u32[]{:S(2)}) copy-start(bf16[256,128,128]{2,1,0:T(8,128)(2,1)} %refs_3_.3) | copy-start | bytes 25165828
  3.2 55.7 %copy-start.3 = (s32[256]{0:T(256)S(1)}, s32[256]{0:T(256)}, u32[]{:S(2)}) copy-start(s32[256]{0:T(256)} %refs_0_.3) | copy-start | bytes 3076
  3.2 55.7 %copy-start.4 = (s32[256]{0:T(256)S(1)}, s32[256]{0:T(256)}, u32[]{:S(2)}) copy-start(s32[256]{0:T(256)} %refs_1_.3) | copy-start | bytes 3076
  124.8 3.4 %copy-start.1 = (bf16[256,128,128]{2,1,0:T(8,128)(2,1)S(1)}, bf16[256,128,128]{2,1,0:T(8,128)(2,1)}, u32[]{:S(2)}) copy-start(bf16[256,128,128]{2,1,0:T(8,128)(2,1)} %refs_3_.3) | copy-start | bytes 25165828
  160.4 0.8 copy-start.2

commit v7 on v6

--- a/solution.py
+++ b/solution.py
@@ -333,12 +333,23 @@
 def project_kernel(nb, *refs):
     y_ref, c_ref = refs[:2]
     basis = refs[2:2 + nb]
-    z_ref, g_ref, ok_ref = refs[2 + nb:5 + nb]
-    scratch = refs[5 + nb:]
+    rest = refs[2 + nb:]
+    if nb == 2:
+        rot_ref, z_ref, g_ref, ok_ref, part_ref = rest[:5]
+        scratch = rest[5:]
+    else:
+        z_ref, g_ref, ok_ref = rest[:3]
+        scratch = rest[3:]
+
+    def during():
+        if nb == 2:
+            rot = rot_ref[...]
+            put_wide(part_ref, nn(rot[:, 0:64], wide(basis[0])) + nn(rot[:, 64:128], wide(basis[1])))
+
     greet()
     scratch[0][...] = c_ref[...]
     greeted()
-    c = total(scratch) * (1.0 / NODES)
+    c = total(scratch, during) * (1.0 / NODES)
     whole = unfold(c[32 * nb:])
     g = whole
     z = wide(y_ref)
@@ -381,21 +392,28 @@
     o_ref[...] = total(scratch) * (1.0 / NODES)
 
 
-def last_kernel(z_ref, g_ref, q0_ref, q1_ref, rot_ref, o_ref):
-    rot = rot_ref[...]
+def last_kernel(z_ref, g_ref, rot_ref, part_ref, o_ref):
     m = inverse_factor(unfold(g_ref[...]))
-    tail = nn(rot[:, 128:192], m)
-    o = nn(rot[:, 0:64], wide(q0_ref)) + nn(rot[:, 64:128], wide(q1_ref)) + nn(tail, wide(z_ref))
-    put_wide(o_ref, o)
+    tail = nn(rot_ref[:, 128:192], m)
+    put_wide(o_ref, wide(part_ref) + nn(tail, wide(z_ref)))
 
 
 def apply_kernel(nb, *refs):
     rows, cols, count, values, p_ref, h_ref = refs[:6]
     basis = refs[6:6 + nb]
-    y_ref, c_ref, src, acc, swap = refs[6 + nb:]
+    y_ref, c_ref, src, acc, swap, buf, sem = refs[6 + nb:]
     n = count[0]
     nchunk = (n + CHUNK - 1) // CHUNK
 
+    def fetch(c):
+        part = pl.ds(c * CHUNK, CHUNK)
+        return pltpu.make_async_copy(values.at[part], buf.at[part], sem.at[c])
+
+    def begin(c, carry):
+        fetch(c).start()
+        return carry
+
+    lax.fori_loop(0, nchunk, begin, 0)
     acc[...] = jnp.zeros_like(acc)
     src[0:RT] = p_ref[...]
     swap[...] = swap_matrix()
@@ -413,11 +431,12 @@
     lax.fori_loop(0, 8, unpack, 0)
 
     def step(c, carry):
+        fetch(c).wait()
         for u in range(CHUNK):
             k = c * CHUNK + u
             r = jnp.where(k < n, rows[k], RT)
             acc[r] += lax.dot_general(
-                src[cols[k]], values[k], (((1,), (1,)), ((), ())), preferred_element_type=F32
+                src[cols[k]], buf[k], (((1,), (1,)), ((), ())), preferred_element_type=F32
             )
         return carry
 
@@ -450,12 +469,14 @@
     return pl.pallas_call(
         functools.partial(apply_kernel, nb),
         out_shape=(block(F32), jax.ShapeDtypeStruct((32 * nb + 32, 128), F32)),
-        in_specs=[SMEM] * 3 + [VMEM] * (3 + nb),
+        in_specs=[SMEM] * 3 + [pl.BlockSpec(memory_space=pl.ANY)] + [VMEM] * (2 + nb),
         out_specs=(VMEM,) * 2,
         scratch_shapes=[
             pltpu.VMEM((80, BLK, TILE), BF16),
             pltpu.VMEM((RT + 1, BLK, TILE), F32),
             pltpu.VMEM((512, 512), BF16),
+            pltpu.VMEM((DEVS, TILE, TILE), BF16),
+            pltpu.SemaphoreType.DMA((DEVS // CHUNK,)),
         ],
         compiler_params=pltpu.CompilerParams(vmem_limit_bytes=24 * 1024 * 1024),
     )(rows, cols, count, values, p, halo, *basis)
@@ -463,6 +484,7 @@
 
 def body(start, values, rows, cols, count, send_rows, send_count, rotation):
     state = (block(F32), block(BF16), jax.ShapeDtypeStruct((DEVS, 16, 128), BF16))
+    values = pltpu.with_memory_space_constraint(values, pltpu.HBM)
     table = jax.ShapeDtypeStruct((64, 128), jnp.int32)
     q0, p, halo, lsel, tsel = remote(
         first_kernel, 1, state + (table, table), sum_scratch(32) + halo_scratch(), start, send_rows[0], send_count
@@ -478,7 +500,8 @@
 
     q1, p, halo = lax.cond(ok[0, 0] > 0, fast, slow, z, g, lsel, tsel)
     y, c = apply_graph(rows, cols, count, values, p, halo, [q0, q1])
-    z, g, ok = project(5, y, c, [q0, q1])
+    turned = rotation.T
+    z, g, ok, part = project(5, y, c, [q0, q1], turned)
     small = (jax.ShapeDtypeStruct((32, 128), F32),)
     g = lax.cond(
         ok[0, 0] > 0, lambda z, g: g, lambda z, g: remote(gram_kernel, 6, small, sum_scratch(32), z, g)[0], z, g
@@ -486,16 +509,17 @@
     return pl.pallas_call(
         last_kernel,
         out_shape=block(F32),
-        in_specs=[VMEM] * 5,
+        in_specs=[VMEM] * 4,
         out_specs=VMEM,
         compiler_params=pltpu.CompilerParams(vmem_limit_bytes=24 * 1024 * 1024),
-    )(z, g, q0, q1, rotation.T)
-
-
-def project(cid, y, c, basis):
+    )(z, g, turned, part)
+
+
+def project(cid, y, c, basis, *more):
     nb = len(basis)
     outs = (block(F32), jax.ShapeDtypeStruct((32, 128), F32), jax.ShapeDtypeStruct((8, 128), jnp.int32))
-    return remote(functools.partial(project_kernel, nb), cid, outs, sum_scratch(32 * nb + 32), y, c, *basis)
+    outs += (block(F32),) * len(more)
+    return remote(functools.partial(project_kernel, nb), cid, outs, sum_scratch(32 * nb + 32), y, c, *basis, *more)
 
 
 def solution(mesh):

time: 168 us -> 164 us (0.976)
  local copies, waits for them, and re-layouts: 7.8 us -> 3.61 us
    pallas_call x2, Pallas kernels: 10.8 us -> 19.6 us  [apply_graph(): pl.pallas_call(functools.partial(apply_kernel, nb), out_shape=(block(F32)...]
    pallas_call x4, Pallas kernels: 141 us -> 133 us  [remote(): pl.pallas_call(kernel, out_shape=outs, in_specs=[VMEM] * len(operands), o...]
    unnamed x15 -> x11, local copies, waits for them, and re-layouts: 6.77 us -> 2.58 us
where the time goes in v7:
time: 164 us; the launch traced here: 163 us
  Pallas kernels  157 us (96%)
  local copies, waits for them, and re-layouts  3.61 us (2%)
  between operations  2.06 us (1%)
    pallas_call x4, Pallas kernels, remote(): pl.pallas_call(kernel, out_shape=outs, in_specs=[VMEM] * len(operands), o...  133 us
    pallas_call x2, Pallas kernels, apply_graph(): pl.pallas_call(functools.partial(apply_kernel, nb), out_shape=(block(F32)...  19.6 us
    pallas_call x1, Pallas kernels, body(): pl.pallas_call(last_kernel, out_shape=block(F32), in_specs=[VMEM] * 4, ou...  5.11 us

profile of v7, /device:TPU:1, one launch (start us, length us, event | category | flops | bytes accessed | tf_op | source)
XLA Modules:
  0.0 163.0 jit_solution(5295113966388594170)
XLA Ops:
  0.7 0.9 copy.9
  1.5 0.0 copy-start.3
  1.5 1.0 copy-done.3
  2.6 0.0 copy-start.4
  2.6 0.7 copy-done.4
  3.2 0.0 copy-start.1
  3.2 0.0 copy-start.2
  3.2 55.6 %shard_map.82 = (f32[16,64,128]{2,1,0:T(8,128)S(1)}, bf16[16,64,128]{2,1,0:T(8,128)(2,1)S(1)}, bf16[256,16,128]{2,1,0:T(8,128)(2,1)S(1)}, s32[64,128]{1,0:T(8,128)S(1)}, s32[64,128]{1,0:T(8,128)S(1)}) custom-call(f32[16,64,128]{2,1,0:T(8,128)S(1)} %copy-done.3, s32[256,32]{1,0:T(8,128)S(1)} %bitcast.4, s32[1,256]{1,0:T(1,128)S(1)} %copy-done.4), custom_call_target="tpu_custom_call" | custom-call | flops 20000000000 | bytes 100000000 | tf_op jit(solution)/shard_map/pallas_call | solution.py:454
  58.9 0.0 copy-done.1
  58.9 0.0 copy-done.2
  58.9 9.5 %shard_map.83 = (f32[16,64,128]{2,1,0:T(8,128)S(1)}, f32[64,128]{1,0:T(8,128)S(1)}) custom-call(s32[256]{0:T(256)S(1)} %copy-done.1, s32[256]{0:T(256)S(1)} %copy-done.2, s32[1]{0:T(128)S(6)} %copy.19.refs_2_, bf16[256,128,128]{2,1,0:T(8,128)(2,1)} %refs_3_.3, bf16[16,64,128]{2,1,0:T(8,128)(2,1)S(1)} %get-tuple-element.58.refs_4_, ...), custom_call_target="tpu_custom_call" | custom-call | tf_op jit(solution)/shard_map/pallas_call | solution.py:469
  68.4 20.1 %shard_map.84 = (f32[16,64,128]{2,1,0:T(8,128)S(1)}, f32[32,128]{1,0:T(8,128)S(1)}, s32[8,128]{1,0:T(8,128)S(1)}) custom-call(f32[16,64,128]{2,1,0:T(8,128)S(1)} %get-tuple-element.61.refs_0_, f32[64,128]{1,0:T(8,128)S(1)} %get-tuple-element.62.refs_1_, f32[16,64,128]{2,1,0:T(8,128)S(1)} %get-tuple-element.60.refs_6_.refs_2_), custom_call_target="tpu_custom_call" | custom-call | flops 20000000000 | bytes 100000000 | tf_op jit(solution)/shard_map/pallas_call | solution.py:454
  88.5 0.5 slice.6
  89.7 36.6 %conditional.2 = ((f32[16,64,128]{2,1,0:T(8,128)S(1)}, bf16[16,64,128]{2,1,0:T(8,128)(2,1)S(1)}, bf16[256,16,128]{2,1,0:T(8,128)(2,1)S(1)})) conditional(s32[]{:T(128)} %bitcast.1, (f32[16,64,128]{2,1,0:T(8,128)S(1)}, f32[32,128]{1,0:T(8,128)S(1)}, s32[64,128]{1,0:T(8,128)S(1)}, s32[64,128]{1,0:T(8,128)S(1)}) %tuple.17, ...), branch_computations={%region_0.0_spmd, %region_1.0_spmd} | conditional | flops 20000000000 | bytes 100000008 | solution.py:501
  89.7 36.6 %branch_1_fun.1 = (f32[16,64,128]{2,1,0:T(8,128)S(1)}, bf16[16,64,128]{2,1,0:T(8,128)(2,1)S(1)}, bf16[256,16,128]{2,1,0:T(8,128)(2,1)S(1)}) custom-call(f32[16,64,128]{2,1,0:T(8,128)S(1)} %get-tuple-element.33.z_ref, f32[32,128]{1,0:T(8,128)S(1)} %get-tuple-element.34.g_ref, s32[64,128]{1,0:T(8,128)S(1)} %get-tuple-element.35.l_ref, ...), custom_call_target="tpu_custom_call" | custom-call | flops 20000000000 | bytes 100000000 | tf_op jit(solution)/shard_map/cond/branch_1_fun/pallas_call | solution.py:454
  126.3 0.0 copy-start
  126.3 10.1 %shard_map.85 = (f32[16,64,128]{2,1,0:T(8,128)S(1)}, f32[96,128]{1,0:T(8,128)S(1)}) custom-call(s32[256]{0:T(256)S(1)} %copy-done.1, s32[256]{0:T(256)S(1)} %copy-done.2, s32[1]{0:T(128)S(6)} %copy.19.refs_2_, bf16[256,128,128]{2,1,0:T(8,128)(2,1)} %refs_3_.3, bf16[16,64,128]{2,1,0:T(8,128)(2,1)S(1)} %get-tuple-element.68.refs_4_, ...), custom_call_target="tpu_custom_call" | custom-call | tf_op jit(solution)/shard_map/pallas_call | solution.py:469
  136.4 0.0 copy-done
  136.5 20.2 %shard_map.86 = (f32[16,64,128]{2,1,0:T(8,128)S(1)}, f32[32,128]{1,0:T(8,128)S(1)}, s32[8,128]{1,0:T(8,128)S(1)}, f32[16,64,128]{2,1,0:T(8,128)S(1)}) custom-call(f32[16,64,128]{2,1,0:T(8,128)S(1)} %get-tuple-element.71.refs_0_, f32[96,128]{1,0:T(8,128)S(1)} %get-tuple-element.72.refs_1_, f32[16,64,128]{2,1,0:T(8,128)S(1)} %get-tuple-element.60.refs_6_.refs_2_, ...), custom_call_target="tpu_custom_call" | custom-call | flops 20000000000 | bytes 100000000 | tf_op jit(solution)/shard_map/pallas_call | solution.py:454
  156.7 0.5 slice.7
  157.9 5.1 %shard_map.87 = f32[16,64,128]{2,1,0:T(8,128)} custom-call(f32[16,64,128]{2,1,0:T(8,128)S(1)} %get-tuple-element.73.z_ref, f32[32,128]{1,0:T(8,128)S(1)} %get-tuple-element.84.g_ref, f32[64,192]{1,0:T(8,128)S(1)} %bitcast.6, f32[16,64,128]{2,1,0:T(8,128)S(1)} %get-tuple-element.76.part_ref), custom_call_target="tpu_custom_call" | custom-call | tf_op jit(solution)/shard_map/pallas_call | solution.py:509
  (1 shorter events, 0.0 us)
Async XLA Ops:
  1.5 1.0 copy-start.3
  2.6 0.7 copy-start.4
  3.2 55.6 %copy-start.1 = (s32[256]{0:T(256)S(1)}, s32[256]{0:T(256)}, u32[]{:S(2)}) copy-start(s32[256]{0:T(256)} %refs_0_.3) | copy-start | bytes 3076
  3.2 55.6 %copy-start.2 = (s32[256]{0:T(256)S(1)}, s32[256]{0:T(256)}, u32[]{:S(2)}) copy-start(s32[256]{0:T(256)} %refs_1_.3) | copy-start | bytes 3076
  126.3 10.1 %copy-start = (f32[192,64]{0,1:T(8,128)S(1)}, f32[192,64]{0,1:T(8,128)}, u32[]{:S(2)}) copy-start(f32[192,64]{0,1:T(8,128)} %param.19) | copy-start | bytes 147460
